TPU v7x, 128 devices: a whole 4x4x4 slice. The times are simulated.
128 devices in a mesh: gx: 4 (over y), gy: 32 (over z, x, core).
Axes of the slice: x: 4, y: 4, z: 4, core: 2. Of those that a mesh axis runs over, the one named last changes fastest.
Arguments:
- fine_state: bfloat16 [32768, 256], P(('gx', 'gy')), may hold values from -6 to 6
- coarse_state: bfloat16 [8192, 256], P('gy'), may hold values from -6 to 6
- up_target: int32 [65536], P(('gx', 'gy')), may hold values from 0 to 255
- down_source: int32 [98304], P(('gx', 'gy')), may hold values from 0 to 255
- halo_lists: int32 [64, 128], P('gy'), may hold values from 0 to 255
- same_source: int32 [49152], P('gy'), may hold values from 0 to 511, as said below
- matrices: bfloat16 [3, 6, 256, 256], replicated, may hold values from -0.375 to 0.375
- biases: float32 [3, 4, 256], replicated, may hold values from -3 to 3
- fine_cotangent: bfloat16 [32768, 256], P(('gx', 'gy')), may hold values from -6 to 6
Outputs:
- fine_out: bfloat16 [32768, 256], P(('gx', 'gy'))
- lifted_cotangent: float32 [8192, 256], P('gy')
- grad_matrices: float32 [3, 6, 256, 256], replicated
- grad_biases: float32 [3, 4, 256], replicated
Inputs may be any that keep to these rules, and one draw needn't show every extreme that they name: `up_target`: entry n * 2 + k is the in-sector index, among the 256 coarse nodes of fine node n's sector, of the receiver of fine node n's k-th up edge. `down_source`: entry n * 3 + k is the in-sector index, among the 256 coarse nodes of fine node n's sector, of the sender of fine node n's k-th down edge. `halo_lists`: row 2 j lists in-sector indices of coarse nodes of sector j read by sector j - 1, row 2 j + 1 those read by sector j + 1; sectors wrap around; entries may repeat. `same_source`: entry c * 6 + k is a row of the extended block of coarse node c's sector: below 128 a row passed by the previous sector, from 128 to 383 the sector's own node of that index minus 128, above that a row passed by the next sector.
All inputs are finite; a program needn't handle non-finite values.
Results may differ from a plain program's by a relative error of at most 0.025.
Values may be sent and summed in bfloat16 or wider, within the bound.
A program may use at most 128 MiB of HBM per device.

v0:
```python
import math

import jax
import jax.numpy as jnp
from jax import lax
from jax.sharding import PartitionSpec as P


def with_halo(shard, sides, width):
    for axis, dim in sides:
        size, length = (lax.axis_size(axis), shard.shape[dim])
        up = [(i, (i + 1) % size) for i in range(size)]
        down = [(j, i) for i, j in up]
        last = lax.slice_in_dim(shard, length - width, length, axis=dim)
        leading = lax.slice_in_dim(shard, 0, width, axis=dim)
        before = lax.ppermute(last, axis, up)
        after = lax.ppermute(leading, axis, down)
        shard = jnp.concatenate([before, shard, after], axis=dim)
    return shard


def layer_norm(values):
    centre = jnp.mean(values, axis=-1, keepdims=True)
    centred = values - centre
    spread = jnp.mean(centred * centred, axis=-1, keepdims=True)
    return centred * lax.rsqrt(spread + 1e-05)


def dot_plain(left_side, right_side):
    return jnp.dot(left_side, right_side, preferred_element_type=jnp.float32)


def dot_rows(left_side, right_side):
    return lax.dot_general(
        left_side, right_side, (((0,), (0,)), ((), ())), preferred_element_type=jnp.float32
    )


def dot_cols(left_side, right_side):
    return lax.dot_general(
        left_side, right_side, (((1,), (1,)), ((), ())), preferred_element_type=jnp.float32
    )


def silu_back(at_point, cotangent):
    return jax.vjp(jax.nn.silu, at_point)[1](cotangent)[0]


def norm_back(at_point, cotangent):
    return jax.vjp(layer_norm, at_point)[1](cotangent)[0]


def edge_forward(summed, w_second, b_first, b_second):
    shifted = summed + b_first
    active = jax.nn.silu(shifted).astype(jnp.bfloat16)
    inner_sum = dot_plain(active, w_second) + b_second
    return (layer_norm(inner_sum), (shifted, active, inner_sum))


def edge_backward(grad_message, stored, w_second):
    shifted, active, inner_sum = stored
    grad_inner = norm_back(inner_sum, grad_message)
    inner_half = grad_inner.astype(jnp.bfloat16)
    grad_weight = dot_rows(active, inner_half)
    grad_shift = silu_back(shifted, dot_cols(inner_half, w_second))
    return (grad_shift, grad_weight, jnp.sum(grad_shift, axis=0), jnp.sum(grad_inner, axis=0))


def node_forward(state, gathered, w_self, w_agg, w_out, b_third, b_fourth):
    agg_half = gathered.astype(jnp.bfloat16)
    inner_sum = dot_plain(state, w_self) + dot_plain(agg_half, w_agg) + b_third
    active = jax.nn.silu(inner_sum).astype(jnp.bfloat16)
    outer_sum = dot_plain(active, w_out) + b_fourth
    result = (state.astype(jnp.float32) + layer_norm(outer_sum)).astype(jnp.bfloat16)
    return (result, (agg_half, inner_sum, active, outer_sum))


def node_backward(grad_result, state, stored, w_self, w_agg, w_out, want_state):
    agg_half, inner_sum, active, outer_sum = stored
    grad_outer = norm_back(outer_sum, grad_result)
    outer_half = grad_outer.astype(jnp.bfloat16)
    grad_wout = dot_rows(active, outer_half)
    grad_inner = silu_back(inner_sum, dot_cols(outer_half, w_out))
    inner_half = grad_inner.astype(jnp.bfloat16)
    grad_wself = dot_rows(state, inner_half)
    grad_wagg = dot_rows(agg_half, inner_half)
    grad_agg = dot_cols(inner_half, w_agg)
    grad_state = None
    if want_state:
        grad_state = grad_result + dot_cols(inner_half, w_self)
    return (
        grad_state,
        grad_agg,
        (grad_wself, grad_wagg, grad_wout),
        (jnp.sum(grad_inner, axis=0), jnp.sum(grad_outer, axis=0)),
    )


def same_edges(extended, own_rows, sources, w_send, w_recv, w_second, b_first, b_second):
    feature_width = own_rows.shape[1]
    node_count = own_rows.shape[0]
    sent_rows = dot_plain(extended, w_send)
    taken_rows = dot_plain(own_rows, w_recv)
    summed = (
        sent_rows[sources].reshape(node_count, -1, feature_width) + taken_rows[:, None, :]
    ).reshape(-1, feature_width)
    message, stored = edge_forward(summed, w_second, b_first, b_second)
    return (message.reshape(node_count, -1, feature_width).sum(1), stored)


def lend_rows(coarse_lifted, halo_lists):
    payload = jnp.stack([coarse_lifted[halo_lists[0]], coarse_lifted[halo_lists[1]]])
    padded = with_halo(payload, (("gy", 0),), 1)
    return jnp.concatenate([padded[0], coarse_lifted, padded[3]], axis=0)


def return_rows(grad_extended, halo_lists, rows_coarse, halo_rows):
    lent_back = jnp.stack([grad_extended[:halo_rows], grad_extended[halo_rows + rows_coarse :]])
    returned = with_halo(lent_back.astype(jnp.bfloat16), (("gy", 0),), 1).astype(lent_back.dtype)
    grad_sent_one = grad_extended[halo_rows : halo_rows + rows_coarse]
    return grad_sent_one.at[halo_lists[0]].add(returned[0]).at[halo_lists[1]].add(returned[3])


def local(
    fine_state,
    coarse_state,
    up_target,
    down_source,
    halo_lists,
    same_source,
    matrices,
    biases,
    fine_cotangent,
):
    rows_fine, feature_width = fine_state.shape
    rows_coarse = coarse_state.shape[0]
    halo_rows = halo_lists.shape[1]
    total_fine = rows_fine * lax.axis_size("gx") * lax.axis_size("gy")
    layer_zero, bias_zero = (matrices[0], biases[0])
    layer_one, bias_one = (matrices[1], biases[1])
    layer_two, bias_two = (matrices[2], biases[2])
    sent_zero = dot_plain(fine_state, layer_zero[0])
    taken_zero = dot_plain(coarse_state, layer_zero[1])
    up_summed = (
        sent_zero[:, None, :] + taken_zero[up_target].reshape(rows_fine, -1, feature_width)
    ).reshape(-1, feature_width)
    up_message, up_stored = edge_forward(up_summed, layer_zero[2], bias_zero[0], bias_zero[1])
    up_partial = jax.ops.segment_sum(up_message, up_target, num_segments=rows_coarse)
    up_total = lax.psum(up_partial.astype(jnp.bfloat16), "gx").astype(jnp.float32)
    coarse_lifted, node_zero = node_forward(
        coarse_state,
        up_total,
        layer_zero[3],
        layer_zero[4],
        layer_zero[5],
        bias_zero[2],
        bias_zero[3],
    )
    extended = lend_rows(coarse_lifted, halo_lists)
    gathered_one, same_stored = same_edges(
        extended,
        coarse_lifted,
        same_source,
        layer_one[0],
        layer_one[1],
        layer_one[2],
        bias_one[0],
        bias_one[1],
    )
    coarse_mixed, node_one = node_forward(
        coarse_lifted,
        gathered_one,
        layer_one[3],
        layer_one[4],
        layer_one[5],
        bias_one[2],
        bias_one[3],
    )
    sent_two = dot_plain(coarse_mixed, layer_two[0])
    taken_two = dot_plain(fine_state, layer_two[1])
    down_summed = (
        sent_two[down_source].reshape(rows_fine, -1, feature_width) + taken_two[:, None, :]
    ).reshape(-1, feature_width)
    down_message, down_stored = edge_forward(down_summed, layer_two[2], bias_two[0], bias_two[1])
    gathered_two = down_message.reshape(rows_fine, -1, feature_width).sum(1)
    fine_out, node_two = node_forward(
        fine_state, gathered_two, layer_two[3], layer_two[4], layer_two[5], bias_two[2], bias_two[3]
    )
    grad_result = fine_cotangent.astype(jnp.float32) * (1.0 / math.sqrt(total_fine))
    unused, grad_two_agg, node_two_w, node_two_b = node_backward(
        grad_result, fine_state, node_two, layer_two[3], layer_two[4], layer_two[5], False
    )
    down_count = down_source.shape[0] // rows_fine
    down_grad_message = jnp.broadcast_to(
        grad_two_agg[:, None, :], (rows_fine, down_count, feature_width)
    ).reshape(-1, feature_width)
    down_grad, down_second, down_bfirst, down_bsecond = edge_backward(
        down_grad_message, down_stored, layer_two[2]
    )
    grad_taken_two = down_grad.reshape(rows_fine, -1, feature_width).sum(1)
    grad_recv_two = dot_rows(fine_state, grad_taken_two.astype(jnp.bfloat16))
    sent_partial = jax.ops.segment_sum(down_grad, down_source, num_segments=rows_coarse)
    sent_own = lax.psum(sent_partial.astype(jnp.bfloat16), "gx").astype(jnp.float32)
    own_count = sent_own.shape[0]
    sent_half = sent_own.astype(jnp.bfloat16)
    grad_send_two = dot_rows(coarse_mixed, sent_half)
    grad_mixed = dot_cols(sent_half, layer_two[0])
    grad_lifted, grad_one_agg, node_one_w, node_one_b = node_backward(
        grad_mixed, coarse_lifted, node_one, layer_one[3], layer_one[4], layer_one[5], True
    )
    same_count = same_source.shape[0] // own_count
    same_grad_message = jnp.broadcast_to(
        grad_one_agg[:, None, :], (own_count, same_count, feature_width)
    ).reshape(-1, feature_width)
    same_grad, same_second, same_bfirst, same_bsecond = edge_backward(
        same_grad_message, same_stored, layer_one[2]
    )
    grad_taken_one = same_grad.reshape(own_count, -1, feature_width).sum(1)
    grad_extended = jax.ops.segment_sum(
        same_grad, same_source, num_segments=rows_coarse + 2 * halo_rows
    )
    grad_sent_one = return_rows(grad_extended, halo_lists, rows_coarse, halo_rows)
    taken_one_half = grad_taken_one.astype(jnp.bfloat16)
    sent_one_half = grad_sent_one.astype(jnp.bfloat16)
    grad_recv_one = dot_rows(coarse_lifted, taken_one_half)
    grad_send_one = dot_rows(coarse_lifted, sent_one_half)
    grad_lifted = (
        grad_lifted + dot_cols(taken_one_half, layer_one[1]) + dot_cols(sent_one_half, layer_one[0])
    )
    lifted_cotangent = grad_lifted * math.sqrt(total_fine)
    unused, grad_zero_agg, node_zero_w, node_zero_b = node_backward(
        grad_lifted, coarse_state, node_zero, layer_zero[3], layer_zero[4], layer_zero[5], False
    )
    up_grad_message = grad_zero_agg[up_target]
    up_grad, up_second, up_bfirst, up_bsecond = edge_backward(
        up_grad_message, up_stored, layer_zero[2]
    )
    grad_send_zero = dot_rows(
        fine_state, up_grad.reshape(rows_fine, -1, feature_width).sum(1).astype(jnp.bfloat16)
    )
    grad_recv_zero = dot_rows(coarse_state[up_target], up_grad.astype(jnp.bfloat16))
    replica_mask = (lax.axis_index("gx") == 0).astype(jnp.float32)
    local_matrices = jnp.stack(
        [
            jnp.stack(
                [
                    grad_send_zero,
                    grad_recv_zero,
                    up_second,
                    replica_mask * node_zero_w[0],
                    replica_mask * node_zero_w[1],
                    replica_mask * node_zero_w[2],
                ]
            ),
            replica_mask
            * jnp.stack(
                [
                    grad_send_one,
                    grad_recv_one,
                    same_second,
                    node_one_w[0],
                    node_one_w[1],
                    node_one_w[2],
                ]
            ),
            jnp.stack(
                [
                    replica_mask * grad_send_two,
                    grad_recv_two,
                    down_second,
                    node_two_w[0],
                    node_two_w[1],
                    node_two_w[2],
                ]
            ),
        ]
    )
    local_biases = jnp.stack(
        [
            jnp.stack(
                [
                    up_bfirst,
                    up_bsecond,
                    replica_mask * node_zero_b[0],
                    replica_mask * node_zero_b[1],
                ]
            ),
            replica_mask * jnp.stack([same_bfirst, same_bsecond, node_one_b[0], node_one_b[1]]),
            jnp.stack([down_bfirst, down_bsecond, node_two_b[0], node_two_b[1]]),
        ]
    )
    grad_matrices, grad_biases = lax.psum((local_matrices, local_biases), ("gx", "gy"))
    return (fine_out, lifted_cotangent, grad_matrices, grad_biases)


def solution(mesh):
    in_specs = (
        P(("gx", "gy"), None),
        P("gy", None),
        P(("gx", "gy")),
        P(("gx", "gy")),
        P("gy", None),
        P("gy"),
        P(),
        P(),
        P(("gx", "gy"), None),
    )
    out_specs = (P(("gx", "gy"), None), P("gy", None), P(), P())
    return jax.shard_map(local, mesh=mesh, in_specs=in_specs, out_specs=out_specs, check_vma=False)
```

profile of v0, /device:TPU:1, one launch (start us, length us, event | category | flops | bytes accessed | tf_op | source)
XLA Modules:
  0.0 419.8 jit_solution(10282470678205091986)
XLA Ops:
  12.6 1.6 gather_fusion
  17.6 3.6 scatter_custom_fusion
  24.3 1.8 fusion.113
  29.1 35.3 %all-reduce.4.cloned.1.call-done = bf16[256,256]{1,0:T(8,128)(2,1)} async-done(((bf16[256,256]{1,0:T(8,128)(2,1)}), bf16[256,256]{1,0:T(8,128)(2,1)}) %all-reduce.4.cloned.1.call-update) | async-done | bytes 131088 | tf_op jit(solution)/shard_map/psum | solution.py:149
  67.7 1.8 fusion.87
  71.5 2.8 collective-permute-start.1
  74.3 1.6 collective-permute-start
  76.0 1.8 fusion.92
  79.2 4.7 %gather_fusion.3 = f32[1536,256]{1,0:T(8,128)} fusion(f32[512,256]{1,0:T(8,128)S(1)} %fusion.41, s32[2048]{0:T(1024)S(1)} %pad_clamp_fusion), kind=kCustom, calls=%fused_computation.3 | custom fusion | bytes 3151872 | tf_op jit(solution)/shard_map/gather | solution.py:105
  85.3 1.6 multiply_convert_fusion
  88.1 1.6 fusion.197
  91.9 1.5 reshape.560
  93.5 2.3 reduce_sum.370
  100.2 2.9 gather_fusion.4
  103.1 1.5 gather.34
  111.8 1.9 reduce_sum.378
  117.1 1.8 fusion.201
  121.2 1.6 reshape.562
  124.9 1.9 fusion.202
  126.8 6.0 %scatter_custom_fusion.1 = f32[256,256]{1,0:T(8,128)S(1)} fusion(s32[768]{0:T(1024)} %param.12, f32[768,256]{1,0:T(8,128)S(1)} %get-tuple-element.68, f32[]{:T(128)} %constant.74.clone.1), kind=kCustom, calls=%fused_computation.216 | custom fusion | flops 196608 | bytes 262656 | tf_op jit(solution)/shard_map/scatter-add | solution.py:202
  133.6 2.6 gather_fusion.6
  139.0 2.6 add.495
  144.5 29.6 %all-reduce.6.cloned.1.call-done = bf16[256,256]{1,0:T(8,128)(2,1)} async-done(((bf16[256,256]{1,0:T(8,128)(2,1)}), bf16[256,256]{1,0:T(8,128)(2,1)}) %all-reduce.6.cloned.1.call-update) | async-done | bytes 131088 | tf_op jit(solution)/shard_map/psum | solution.py:203
  176.6 1.8 fusion.193
  178.4 1.9 convolution_add_fusion.5
  182.9 1.6 reshape.563
  187.2 2.4 fusion.203
  190.7 9.0 %scatter_custom_fusion.2 = f32[512,256]{1,0:T(8,128)S(1)} fusion(s32[1536]{0:T(1024)} %param.14, f32[1536,256]{1,0:T(8,128)S(1)} %get-tuple-element.70, f32[]{:T(128)} %constant.74.clone.1), kind=kCustom, calls=%fused_computation.135 | custom fusion | flops 393216 | bytes 524800 | tf_op jit(solution)/shard_map/scatter-add | solution.py:219
  199.8 1.7 reshape.564
  202.1 2.2 fusion.5
  206.3 3.9 collective-permute-start.2
  212.1 2.1 collective-permute-done.3
  214.3 1.7 scatter_custom_fusion.3
  216.0 1.7 scatter_custom_fusion.4
  219.7 1.8 fusion.204
  224.7 1.6 gather_fusion.5
  227.7 2.7 fusion.205
  230.5 2.3 reshape.565
  232.8 2.3 reduce_sum.406
  236.1 3.1 fusion.25
  242.0 1.7 broadcast_multiply_fusion
  247.5 2.6 pad_maximum_fusion
  251.0 2.3 add_reduce_fusion.5
  253.3 1.7 copy.67
  257.0 1.8 copy.68
  259.1 68.5 %psum.31 = f32[3,4,256]{2,1,0:T(4,128)} all-reduce(f32[3,4,256]{2,1,0:T(4,128)S(1)} %pad_maximum_fusion.7), channel_id=1, replica_groups=mesh['gx'=4,'gy'=32] {'gx','gy'}, use_global_device_ids=true, to_apply=%region_49.50 | all-reduce | flops 3072 | bytes 24576 | tf_op jit(solution)/shard_map/psum | solution.py:292
  327.6 79.4 %all-reduce.8.cloned.1.call-done = f32[3,6,256,256]{2,3,1,0:T(8,128)} async-done(((f32[3,6,256,256]{2,3,1,0:T(8,128)}), f32[3,6,256,256]{2,3,1,0:T(8,128)}) %all-reduce.8.cloned.1.call-update) | async-done | bytes 4718608 | tf_op jit(solution)/shard_map/psum | solution.py:292
  407.0 6.0 %copy.69 = f32[3,6,256,256]{3,2,1,0:T(8,128)} copy(f32[3,6,256,256]{2,3,1,0:T(8,128)} %all-reduce.8.cloned.1.call-done) | data formatting | bytes 9437184
  (427 shorter events, 81.6 us)
Async XLA Ops:
  7.2 57.2 %all-reduce.4.cloned.1.call-start = ((), (), s32[]{:S(2)}) async-start(), calls=%async_computation | async-start | bytes 262144 | tf_op jit(solution)/shard_map/psum | solution.py:149
  8.0 6.2 %copy-start.135 = (s32[128]{0:T(128)}, s32[128]{0:T(128)S(1)}, u32[]{:S(2)}) copy-start(s32[128]{0:T(128)S(1)} %get-tuple-element.46) | copy-start | bytes 1540
  8.0 20.5 %copy-start.134 = (s32[128]{0:T(128)}, s32[128]{0:T(128)S(1)}, u32[]{:S(2)}) copy-start(s32[128]{0:T(128)S(1)} %get-tuple-element.47) | copy-start | bytes 1540
  16.6 6.5 %copy-start.94 = (f32[512]{0:T(512)}, f32[512]{0:T(512)S(1)}, u32[]{:S(2)}) copy-start(f32[512]{0:T(512)S(1)} %multiply_reduce_fusion.5) | copy-start | bytes 6148
  16.6 5.4 %copy-start.3 = (bf16[256,256]{1,0:T(8,128)(2,1)S(1)}, bf16[256,256]{1,0:T(8,128)(2,1)}, u32[]{:S(2)}) copy-start(bf16[256,256]{1,0:T(8,128)(2,1)} %param.9) | copy-start | bytes 393220
  17.3 5.8 %copy-start.92 = (f32[512]{0:T(512)}, f32[512]{0:T(512)S(1)}, u32[]{:S(2)}) copy-start(f32[512]{0:T(512)S(1)} %fusion.171) | copy-start | bytes 6148
  17.3 5.8 %copy-start = (bf16[256,256]{1,0:T(8,128)(2,1)S(1)}, bf16[256,256]{1,0:T(8,128)(2,1)}, u32[]{:S(2)}) copy-start(bf16[256,256]{1,0:T(8,128)(2,1)} %param.10) | copy-start | bytes 393220
  17.4 8.8 %copy-start.132 = (s32[768]{0:T(1024)S(1)}, s32[768]{0:T(1024)}, u32[]{:S(2)}) copy-start(s32[768]{0:T(1024)} %param.12) | copy-start | bytes 9220
  17.4 8.7 %copy-start.114 = (s32[1536]{0:T(1024)S(1)}, s32[1536]{0:T(1024)}, u32[]{:S(2)}) copy-start(s32[1536]{0:T(1024)} %param.14) | copy-start | bytes 18436
  17.6 8.7 %copy-start.76 = (bf16[256,256]{1,0:T(8,128)(2,1)S(1)}, bf16[256,256]{1,0:T(8,128)(2,1)}, u32[]{:S(2)}) copy-start(bf16[256,256]{1,0:T(8,128)(2,1)} %param.17) | copy-start | bytes 393220
  21.9 152.1 %all-reduce.6.cloned.1.call-start = ((), (), s32[]{:S(2)}) async-start(), calls=%async_computation.1 | async-start | bytes 262144 | tf_op jit(solution)/shard_map/psum | solution.py:203
  23.1 5.4 %copy-start.18 = (f32[256,256]{1,0:T(8,128)}, f32[256,256]{1,0:T(8,128)S(1)}, u32[]{:S(2)}) copy-start(f32[256,256]{1,0:T(8,128)S(1)} %fusion.67) | copy-start | bytes 786436
  65.6 4.9 %copy-start.68 = (f32[256,256]{1,0:T(8,128)}, f32[256,256]{1,0:T(8,128)S(1)}, u32[]{:S(2)}) copy-start(f32[256,256]{1,0:T(8,128)S(1)} %fusion.14) | copy-start | bytes 786436
  66.9 10.9 %copy-start.87 = (f32[256]{0:T(256)}, f32[256]{0:T(256)S(1)}, u32[]{:S(2)}) copy-start(f32[256]{0:T(256)S(1)} %broadcast_multiply_fusion.10) | copy-start | bytes 3076
  71.5 6.3 %collective-permute-start.1 = (bf16[1,128,256]{1,2,0:T(8,128)(2,1)S(1)}, bf16[1,128,256]{1,2,0:T(8,128)(2,1)S(1)}, u32[]{:S(2)}, u32[]{:S(2)}) collective-permute-start(bf16[1,128,256]{1,2,0:T(8,128)(2,1)S(1)} %bitcast.295), channel_id=1, source_target_pairs={{1,0},{2,1},{3,2},{4,3},{5,4},{6,5},{7,6},{8,7},{9,8},{10,9},{11,1... | collective-permute-start | bytes 196616 | tf_op jit(solution)/shard_map/ppermute | solution.py:17
  74.3 3.6 collective-permute-start
  98.2 4.9 %copy-start.85 = (f32[256]{0:T(256)}, f32[256]{0:T(256)S(1)}, u32[]{:S(2)}) copy-start(f32[256]{0:T(256)S(1)} %broadcast_multiply_fusion.9) | copy-start | bytes 3076
  111.8 4.5 %copy-start.25 = (bf16[256,256]{0,1:T(8,128)(2,1)S(1)}, bf16[256,256]{0,1:T(8,128)(2,1)}, u32[]{:S(2)}) copy-start(bf16[256,256]{0,1:T(8,128)(2,1)} %copy.48) | copy-start | bytes 393220
  124.9 8.7 %copy-start.90 = (s32[1024]{0:T(1024)S(1)}, s32[1024]{0:T(1024)}, u32[]{:S(2)}) copy-start(s32[1024]{0:T(1024)} %copy-done.89) | copy-start | bytes 12292
  126.8 9.4 %copy-start.61 = (f32[768,256]{1,0:T(8,128)}, f32[768,256]{1,0:T(8,128)S(1)}, u32[]{:S(2)}) copy-start(f32[768,256]{1,0:T(8,128)S(1)} %get-tuple-element.68) | copy-start | bytes 2359300
  126.8 9.4 %copy-start.16 = (f32[256,256]{1,0:T(8,128)S(1)}, f32[256,256]{1,0:T(8,128)}, u32[]{:S(2)}) copy-start(f32[256,256]{1,0:T(8,128)} %copy-done.15) | copy-start | bytes 786436
  133.5 273.5 %all-reduce.8.cloned.1.call-start = ((), (), s32[]{:S(2)}) async-start(), calls=%async_computation.2 | async-start | bytes 9437184 | tf_op jit(solution)/shard_map/psum | solution.py:292
  141.6 32.4 %copy-start.9 = (f32[256,256]{0,1:T(8,128)S(1)}, f32[256,256]{0,1:T(8,128)}, u32[]{:S(2)}) copy-start(f32[256,256]{0,1:T(8,128)} %copy-done.8) | copy-start | bytes 786436
  141.6 32.4 %copy-start.86 = (f32[256]{0:T(256)S(1)}, f32[256]{0:T(256)}, u32[]{:S(2)}) copy-start(f32[256]{0:T(256)} %copy-done.85) | copy-start | bytes 3076
  143.1 33.5 %copy-start.72 = (f32[256,256]{1,0:T(8,128)S(1)}, f32[256,256]{1,0:T(8,128)}, u32[]{:S(2)}) copy-start(f32[256,256]{1,0:T(8,128)} %copy-done.71) | copy-start | bytes 786436
  176.6 4.8 %copy-start.51 = (f32[256,256]{0,1:T(8,128)}, f32[256,256]{0,1:T(8,128)S(1)}, u32[]{:S(2)}) copy-start(f32[256,256]{0,1:T(8,128)S(1)} %get-tuple-element.21) | copy-start | bytes 786436
  176.6 6.3 %copy-start.127 = (f32[256]{0:T(256)}, f32[256]{0:T(256)S(1)}, u32[]{:S(2)}) copy-start(f32[256]{0:T(256)S(1)} %negate_multiply_fusion.4) | copy-start | bytes 3076
  206.3 4.6 %copy-start.50 = (f32[256,256]{0,1:T(8,128)S(1)}, f32[256,256]{0,1:T(8,128)}, u32[]{:S(2)}) copy-start(f32[256,256]{0,1:T(8,128)} %convolution_add_fusion.5) | copy-start | bytes 786436
  206.3 5.8 %collective-permute-start.2 = (bf16[1,128,256]{2,1,0:T(8,128)(2,1)S(1)}, bf16[1,128,256]{2,1,0:T(8,128)(2,1)}, u32[]{:S(2)}, u32[]{:S(2)}) collective-permute-start(bf16[1,128,256]{2,1,0:T(8,128)(2,1)S(1)} %get-tuple-element.29), channel_id=1, source_target_pairs={{0,1},{1,2},{2,3},{3,4},{4,5},{5,6},{6,7},{7,8},{8,9},{9,10},{10,1... | collective-permute-start | bytes 196616 | tf_op jit(solution)/shard_map/ppermute | solution.py:16
  210.2 4.1 collective-permute-start.3
  210.9 8.1 %copy-start.46 = (bf16[256,256]{1,0:T(8,128)(2,1)}, bf16[256,256]{1,0:T(8,128)(2,1)S(1)}, u32[]{:S(2)}) copy-start(bf16[256,256]{1,0:T(8,128)(2,1)S(1)} %reduce_sum.398) | copy-start | bytes 393220
  210.9 6.9 %copy-start.11 = (f32[256,256]{0,1:T(8,128)S(1)}, f32[256,256]{0,1:T(8,128)}, u32[]{:S(2)}) copy-start(f32[256,256]{0,1:T(8,128)} %copy-done.10) | copy-start | bytes 786436
  210.9 6.9 %copy-start.88 = (f32[256]{0:T(256)S(1)}, f32[256]{0:T(256)}, u32[]{:S(2)}) copy-start(f32[256]{0:T(256)} %copy-done.87) | copy-start | bytes 3076
  212.1 6.8 %copy-start.108 = (f32[256]{0:T(256)S(1)}, f32[256]{0:T(256)}, u32[]{:S(2)}) copy-start(f32[256]{0:T(256)} %copy-done.107) | copy-start | bytes 3076
  212.1 6.9 %copy-start.111 = (f32[256]{0:T(256)S(1)}, f32[256]{0:T(256)}, u32[]{:S(2)}) copy-start(f32[256]{0:T(256)} %copy-done.110) | copy-start | bytes 3076
  212.1 7.6 %copy-start.69 = (f32[256,256]{1,0:T(8,128)S(1)}, f32[256,256]{1,0:T(8,128)}, u32[]{:S(2)}) copy-start(f32[256,256]{1,0:T(8,128)} %copy-done.68) | copy-start | bytes 786436
  219.7 5.0 %copy-start.91 = (s32[1024]{0:T(1024)S(1)}, s32[1024]{0:T(1024)}, u32[]{:S(2)}) copy-start(s32[1024]{0:T(1024)} %copy-done.89) | copy-start | bytes 12292
  227.1 17.1 %copy-start.112 = (f32[512]{0:T(512)}, f32[512]{0:T(512)S(1)}, u32[]{:S(2)}) copy-start(f32[512]{0:T(512)S(1)} %negate_multiply_fusion.2) | copy-start | bytes 6148
  227.7 8.3 %copy-start.7 = (f32[1536,256]{1,0:T(8,128)S(1)}, f32[1536,256]{1,0:T(8,128)}, u32[]{:S(2)}) copy-start(f32[1536,256]{1,0:T(8,128)} %copy-done.6) | copy-start | bytes 4718596
  230.5 4.6 %copy-start.47 = (bf16[256,256]{1,0:T(8,128)(2,1)S(1)}, bf16[256,256]{1,0:T(8,128)(2,1)}, u32[]{:S(2)}) copy-start(bf16[256,256]{1,0:T(8,128)(2,1)} %copy-done.46) | copy-start | bytes 393220
  230.5 5.6 %copy-start.5 = (f32[1536,256]{1,0:T(8,128)S(1)}, f32[1536,256]{1,0:T(8,128)}, u32[]{:S(2)}) copy-start(f32[1536,256]{1,0:T(8,128)} %gather_fusion.3) | copy-start | bytes 4718596
  230.5 5.6 %copy-start.117 = (f32[1,1,256]{2,1,0:T(1,128)S(1)}, f32[1,1,256]{2,1,0:T(1,128)}, u32[]{:S(2)}) copy-start(f32[1,1,256]{2,1,0:T(1,128)} %get-tuple-element.36) | copy-start | bytes 3076
  236.1 5.0 %copy-start.52 = (f32[256,256]{0,1:T(8,128)S(1)}, f32[256,256]{0,1:T(8,128)}, u32[]{:S(2)}) copy-start(f32[256,256]{0,1:T(8,128)} %copy-done.51) | copy-start | bytes 786436
  236.1 5.0 %copy-start.73 = (f32[256,256]{1,0:T(8,128)S(1)}, f32[256,256]{1,0:T(8,128)}, u32[]{:S(2)}) copy-start(f32[256,256]{1,0:T(8,128)} %copy-done.71) | copy-start | bytes 786436
  236.1 5.0 %copy-start.128 = (f32[256]{0:T(256)S(1)}, f32[256]{0:T(256)}, u32[]{:S(2)}) copy-start(f32[256]{0:T(256)} %copy-done.127) | copy-start | bytes 3076
  250.1 4.9 %copy-start.101 = (f32[768]{0:T(1024)S(1)}, f32[768]{0:T(1024)}, u32[]{:S(2)}) copy-start(f32[768]{0:T(1024)} %copy-done.100) | copy-start | bytes 9220
  250.1 4.9 %copy-start.14 = (f32[768,256]{1,0:T(8,128)S(1)}, f32[768,256]{1,0:T(8,128)}, u32[]{:S(2)}) copy-start(f32[768,256]{1,0:T(8,128)} %copy-done.13) | copy-start | bytes 2359300
  250.8 5.0 %copy-start.53 = (f32[256,256]{0,1:T(8,128)S(1)}, f32[256,256]{0,1:T(8,128)}, u32[]{:S(2)}) copy-start(f32[256,256]{0,1:T(8,128)} %copy-done.51) | copy-start | bytes 786436
  (101 other events, 203.1 us)
Sparse Core Ops, SparseCore 0:
  22.1 42.2 all-reduce.3
  133.7 40.3 all-reduce.5
  250.2 156.7 all-reduce.7
where the time goes:
time: 428 us; the launch traced here: 420 us
  waiting for transfers between devices  147 us (34%)
  local copies, waits for them, and re-layouts  68.5 us (16%)
  blocking collectives  68.5 us (16%)
  matrix products  57.8 us (14%)
  other arithmetic  54 us (13%)
  between operations  15.9 us (4%)
  starting transfers between devices  8.44 us (2%)
    psum x1, waiting for transfers between devices, local(): lax.psum((local_matrices, local_biases), ('gx', 'gy'))  79.4 us
    psum x1, blocking collectives, local(): lax.psum((local_matrices, local_biases), ('gx', 'gy'))  68.5 us
    psum x1, waiting for transfers between devices, local(): lax.psum(up_partial.astype(jnp.bfloat16), 'gx').astype(jnp.float32)  35.3 us
    psum x1, waiting for transfers between devices, local(): lax.psum(sent_partial.astype(jnp.bfloat16), 'gx').astype(jnp.float32)  29.6 us
    dot_general x18, matrix products, dot_plain(): return jnp.dot(left_side, right_side, preferred_element_type=jnp.float32)  23.9 us
    unnamed x291, local copies, waits for them, and re-layouts  23.5 us
    dot_general x13, matrix products, dot_cols(): lax.dot_general(left_side, right_side, (((1,), (1,)), ((), ())), preferre...  21.3 us
    dot_general x18, matrix products, dot_rows(): lax.dot_general(left_side, right_side, (((0,), (0,)), ((), ())), preferre...  12.7 us
  transfers between devices with their start and end apart: 7, of which 5 were waited for; matrix products, arithmetic and copies ran while one was open for 7% of the time, Pallas kernels for 0%

commit v1 on v0

v1 whole, which is shorter than its diff:
```python
import math

import jax
import jax.numpy as jnp
from jax import lax
from jax.experimental import pallas as pl
from jax.experimental.pallas import tpu as pltpu
from jax.sharding import PartitionSpec as P

MESH = pl.DeviceIdType.MESH
F32 = jnp.float32
BF16 = jnp.bfloat16
B = 256
H = 128
UP, DOWN, SAME = (0, 2), (2, 5), (5, 11)
COPIES = 104


def dot_plain(a, b):
    return jnp.dot(a, b, preferred_element_type=F32)


def dot_rows(a, b):
    return lax.dot_general(a, b, (((0,), (0,)), ((), ())), preferred_element_type=F32)


def dot_cols(a, b):
    return lax.dot_general(a, b, (((1,), (1,)), ((), ())), preferred_element_type=F32)


def silu_parts(x):
    gate = 0.5 * jnp.tanh(0.5 * x) + 0.5
    active = x * gate
    return active, gate + active * (1.0 - gate)


def row_mean(x):
    return jnp.mean(x, axis=-1, keepdims=True)


def normed(y):
    centred = y - row_mean(y)
    scale = lax.rsqrt(row_mean(centred * centred) + 1e-05)
    return centred * scale, scale


def norm_back(g, unit, scale):
    return scale * (g - row_mean(g) - unit * row_mean(g * unit))


def col_sum(x):
    return jnp.sum(x, axis=0, keepdims=True)


class Group:
    def __init__(self, post, place, axes, rows, refs, out):
        self.post, self.place, self.axes, self.rows, self.out = post, place, axes, rows, out
        self.g, self.rc, self.s1, self.r1, self.s2, self.r2, self.s3, self.r3, self.s4 = refs
        self.count = rows.stop - rows.start
        self.step = 0
        core = place.core
        self.copies = []
        self.lanes = pl.ds(pl.multiple_of(core * H, H), H)

    def put(self, i, value):
        half = value.astype(BF16)
        self.g[0, i] = half[:, :H]
        self.g[1, i] = half[:, H:]

    def landed(self):
        for copy in self.copies:
            copy.wait_recv()
        self.copies = []

    def advance(self):
        getattr(self, "step%d" % self.step)()
        self.step += 1

    def step0(self):
        other = 1 - self.place.core
        self.copies = [self.post(self.g.at[other], self.rc, self.place.partner())]

    def step1(self):
        self.landed()
        core = self.place.core
        for i in range(self.count):
            self.s1[i] = (self.g[core, i].astype(F32) + self.rc[i].astype(F32)).astype(BF16)
        self.scatter(self.axes[0], 64, self.s1, self.r1)

    def scatter(self, axis, size, src, landing):
        at = self.place.at(axis)
        for d in (1, 2, 3):
            to = lax.rem(at + d, 4)
            rows = pl.ds(pl.multiple_of(to * size, size), size)
            self.copies.append(self.post(src.at[:, rows, :], landing.at[d - 1], self.place.peer(axis, d)))

    def gather_sum(self, axis, size, src, landing, out):
        at = self.place.at(axis)
        rows = pl.ds(pl.multiple_of(at * size, size), size)
        for i in range(self.count):
            total = src[i, rows, :].astype(F32)
            for d in range(3):
                total += landing[d, i].astype(F32)
            out[i] = total.astype(BF16)

    def step2(self):
        self.landed()
        self.gather_sum(self.axes[0], 64, self.s1, self.r1, self.s2)
        self.scatter(self.axes[1], 16, self.s2, self.r2)

    def step3(self):
        self.landed()
        if len(self.axes) == 2:
            self.gather_sum(self.axes[1], 16, self.s2, self.r2, self.s4)
            return
        self.gather_sum(self.axes[1], 16, self.s2, self.r2, self.s3)
        at = self.place.at(self.axes[2])
        for d in (1, 2, 3):
            self.copies.append(self.post(self.s3, self.r3.at[at], self.place.peer(self.axes[2], d)))
        self.r3[at] = self.s3[...]

    def step4(self):
        self.landed()
        if len(self.axes) == 3:
            for i in range(self.count):
                total = self.r3[0, i].astype(F32)
                for j in (1, 2, 3):
                    total += self.r3[j, i].astype(F32)
                self.s4[i] = total.astype(BF16)
        start = self.place.at(self.axes[0]) * 64 + self.place.at(self.axes[1]) * 16
        rows = pl.ds(pl.multiple_of(start, 16), 16)
        spot = self.out.at[self.rows, rows, self.lanes]
        for d in (1, 2, 3):
            self.copies.append(self.post(self.s4, spot, self.place.peer(self.axes[1], d)))
        for i in range(self.count):
            self.out[self.rows.start + i, rows, self.lanes] = self.s4[i]

    def step5(self):
        self.landed()
        rows = pl.ds(pl.multiple_of(self.place.at(self.axes[0]) * 64, 64), 64)
        spot = self.out.at[self.rows, rows, self.lanes]
        for d in (1, 2, 3):
            self.copies.append(self.post(spot, spot, self.place.peer(self.axes[0], d)))

    def step6(self):
        self.landed()
        spot = self.out.at[self.rows, :, self.lanes]
        self.copies = [self.post(spot, spot, self.place.partner())]

    def step7(self):
        self.landed()


class Place:
    def __init__(self):
        self.gx = lax.axis_index("gx")
        self.gy = lax.axis_index("gy")
        self.core = lax.rem(self.gy, 2)
        self.x = lax.rem(self.gy // 2, 4)
        self.z = self.gy // 8

    def at(self, axis):
        return {"x": self.x, "y": self.gx, "z": self.z}[axis]

    def partner(self):
        return (self.gx, self.gy + 1 - 2 * self.core)

    def peer(self, axis, d):
        if axis == "y":
            return (lax.rem(self.gx + d, 4), self.gy)
        if axis == "x":
            return (self.gx, self.z * 8 + lax.rem(self.x + d, 4) * 2 + self.core)
        return (self.gx, lax.rem(self.z + d, 4) * 8 + self.x * 2 + self.core)

    def beside(self, d):
        return (self.gx, lax.rem(self.gy + d + 32, 32))


def deal(source, raw, index, first, end):
    ways = end - first
    raw[:2 * ways, :] = source[...]
    rows = raw[...]
    lane = lax.broadcasted_iota(jnp.int32, rows.shape, 1)
    for k in range(ways):
        place = lane * ways + k
        picked = jnp.take_along_axis(rows, lax.rem(place, H), axis=1, mode="promise_in_bounds")
        line = place[0:1] // H
        for half in (0, 1):
            row = picked[ways * half:ways * half + 1]
            for i in range(1, ways):
                row = jnp.where(line == i, picked[ways * half + i:ways * half + i + 1], row)
            index[first + k:first + k + 1, half * H:half * H + H] = row


def kernel(total_fine, *refs):
    (fine, coarse, cot, up_raw, down_raw, halo_raw, same_raw, mats, bias, fine_out, lifted_cot, grads, gbias) = refs[:13]
    (send_sems, recv_sems, onehot, samehot, act, slope, unit, scale, dys, nact, nslope, nunit, nscale,
     table, ext, gtab, pres, csend, crecv, hsend, hback, node_in, bias_acc, bias_core, bias_slots, raw, index) = refs[13:40]
    group_refs = refs[40:]
    place = Place()
    posted = []

    def post(src, dst, device):
        i = len(posted)
        copy = pltpu.make_async_remote_copy(
            src_ref=src, dst_ref=dst, send_sem=send_sems.at[i], recv_sem=recv_sems.at[i],
            device_id=device, device_id_type=MESH,
        )
        copy.start()
        posted.append(copy)
        return copy

    barrier = pltpu.get_barrier_semaphore()
    near = [place.peer(a, d) for a in ("x", "y", "z") for d in (1, 2, 3)]
    near += [place.partner(), place.beside(1), place.beside(-1)]
    for device in near:
        pl.semaphore_signal(barrier, inc=1, device_id=device, device_id_type=MESH)

    def groups_of(at, axes, rows):
        return Group(post, place, axes, rows, group_refs[9 * at:9 * at + 9], grads)

    edge0 = groups_of(0, ("y", "z", "x"), slice(0, 3))
    node0 = groups_of(1, ("x", "z"), slice(3, 6))
    layer1 = groups_of(2, ("z", "x"), slice(6, 12))
    layer2 = groups_of(3, ("x", "z", "y"), slice(12, 18))

    bias_acc[...] = jnp.zeros_like(bias_acc)
    deal(up_raw, raw, index, *UP)

    def add_bias(row, value):
        bias_acc[row:row + 1, :] += value

    def w(layer, i):
        return mats[layer, i]

    def b(layer, i):
        return bias[layer, i:i + 1, :]

    def hot_rows(block, size):
        nodes = lax.broadcasted_iota(jnp.int32, (size, B), 0)
        return jnp.where(nodes == index[block:block + 1, :], 1.0, 0.0).astype(BF16)

    def edge_forward(block, pre, layer):
        active, slope_now = silu_parts(pre)
        half = active.astype(BF16)
        act[block] = half
        slope[block] = slope_now.astype(BF16)
        message, scale_now = normed(dot_plain(half, w(layer, 2)) + b(layer, 1))
        unit[block] = message.astype(BF16)
        scale[block] = scale_now
        return message

    def edge_backward(block, g, layer):
        dy = norm_back(g, unit[block].astype(F32), scale[block])
        half = dy.astype(BF16)
        dys[block] = half
        dp = slope[block].astype(F32) * dot_cols(half, w(layer, 2))
        return dp, col_sum(dy), col_sum(dp)

    def node_forward(layer, state, agg, pre):
        node_in[layer] = agg
        active, slope_now = silu_parts(pre + dot_plain(agg, w(layer, 4)))
        half = active.astype(BF16)
        nact[layer] = half
        nslope[layer] = slope_now.astype(BF16)
        unit_now, scale_now = normed(dot_plain(half, w(layer, 5)) + b(layer, 3))
        nunit[layer] = unit_now.astype(BF16)
        nscale[layer] = scale_now
        return (state.astype(F32) + unit_now).astype(BF16)

    def node_backward(layer, g, share):
        dz = norm_back(g, nunit[layer].astype(F32), nscale[layer])
        dz16 = dz.astype(BF16)
        dq = nslope[layer].astype(F32) * dot_cols(dz16, w(layer, 5))
        dq16 = dq.astype(BF16)
        add_bias(4 * layer + 3, share * col_sum(dz))
        add_bias(4 * layer + 2, share * col_sum(dq))
        return dz16, dq16

    def sum_start(first, value):
        half = value.astype(BF16)
        csend[first, 0] = half[:H]
        csend[first, 1] = half[H:]
        odd = lax.rem(place.gx, 2)
        one = (place.gx + 1 - 2 * odd, place.gy)
        two = (lax.rem(place.gx + 2 * odd + 3, 4), place.gy)
        waits = [
            post(csend.at[first, 0], crecv.at[first, 0], one),
            post(csend.at[first, 1], crecv.at[first, 1], two),
        ]
        return waits, one, two

    def sum_middle(first, state):
        waits, one, two = state
        for i in (0, 1):
            waits[i].wait_recv()
            both = csend[first, i].astype(F32) + crecv[first, i].astype(F32)
            csend[first + 1, i] = both.astype(BF16)
        return [
            post(csend.at[first + 1, 0], crecv.at[first + 1, 0], two),
            post(csend.at[first + 1, 1], crecv.at[first + 1, 1], one),
        ]

    def sum_end(first, waits):
        parts = []
        for i in (0, 1):
            waits[i].wait_recv()
            both = csend[first + 1, i].astype(F32) + crecv[first + 1, i].astype(F32)
            parts.append(both.astype(BF16))
        return jnp.concatenate(parts, axis=0)

    for block in range(*UP):
        onehot[block] = hot_rows(block, B)
    sent = dot_plain(fine[...], w(0, 0)) + b(0, 0)
    table[...] = dot_plain(coarse[...], w(0, 1)).astype(BF16)
    up_sum = None
    for block in range(*UP):
        message = edge_forward(block, sent + dot_rows(onehot[block], table[...]), 0)
        part = dot_plain(onehot[block], message.astype(BF16))
        up_sum = part if up_sum is None else up_sum + part

    pl.semaphore_wait(barrier, len(near))
    state = sum_start(0, up_sum)
    pres[0] = dot_plain(coarse[...], w(0, 3)) + b(0, 2)
    deal(down_raw, raw, index, *DOWN)
    deal(same_raw, raw, index, *SAME)
    index[11:12, :H] = halo_raw[0:1, :]
    index[11:12, H:] = halo_raw[1:2, :]
    for block in range(*DOWN):
        onehot[block] = hot_rows(block, B)
    onehot[5] = hot_rows(11, B)
    state = sum_middle(0, state)
    for block in range(*SAME):
        samehot[block - 5] = hot_rows(block, 2 * B)
    pres[1] = dot_plain(fine[...], w(2, 3)) + b(2, 2)
    pres[2] = dot_plain(fine[...], w(2, 1)) + b(2, 0)
    agg = sum_end(0, state)
    lifted = node_forward(0, coarse[...], agg, pres[0])
    ext[H:H + B] = lifted
    payload = dot_rows(onehot[5], lifted).astype(BF16)
    hsend[0] = payload[:H]
    hsend[1] = payload[H:]
    halo = [
        post(hsend.at[0], ext.at[H + B:], place.beside(-1)),
        post(hsend.at[1], ext.at[:H], place.beside(1)),
    ]

    pres[3] = dot_plain(lifted, w(1, 1)) + b(1, 0)
    pres[4] = dot_plain(lifted, w(1, 3)) + b(1, 2)
    for copy in halo:
        copy.wait_recv()
    gtab[...] = dot_plain(ext[...], w(1, 0)).astype(BF16)
    same_sum = None
    for block in range(*SAME):
        message = edge_forward(block, pres[3] + dot_rows(samehot[block - 5], gtab[...]), 1)
        same_sum = message if same_sum is None else same_sum + message
    mixed = node_forward(1, ext[H:H + B], same_sum.astype(BF16), pres[4])
    nact[3] = mixed

    table[...] = dot_plain(mixed, w(2, 0)).astype(BF16)
    down_sum = None
    for block in range(*DOWN):
        message = edge_forward(block, pres[2] + dot_rows(onehot[block], table[...]), 2)
        down_sum = message if down_sum is None else down_sum + message
    fine_out[...] = node_forward(2, fine[...], down_sum.astype(BF16), pres[1])
    dz2, dq2 = node_backward(2, cot[...].astype(F32) * (1.0 / math.sqrt(total_fine)), 1.0)
    g = dot_cols(dq2, w(2, 4))
    taken = back = None
    for block in range(*DOWN):
        dp, db2, db1 = edge_backward(block, g, 2)
        add_bias(8, db1)
        add_bias(9, db2)
        part = dot_plain(onehot[block], dp.astype(BF16))
        taken = dp if taken is None else taken + dp
        back = part if back is None else back + part
    state = sum_start(2, back)
    layer2.put(1, dot_rows(fine[...], taken.astype(BF16)))
    layer2.put(2, dot_rows(act[2:5].reshape(3 * B, B), dys[2:5].reshape(3 * B, B)))
    state = sum_middle(2, state)
    layer2.put(3, dot_rows(fine[...], dq2))
    layer2.put(4, dot_rows(node_in[2], dq2))
    layer2.put(5, dot_rows(nact[2], dz2))
    sent_half = sum_end(2, state)
    grad_mixed = dot_cols(sent_half, w(2, 0))
    layer2.put(0, 0.25 * dot_rows(nact[3], sent_half))
    layer2.advance()

    dz1, dq1 = node_backward(1, grad_mixed, 0.25)
    pres[0] = grad_mixed + dot_cols(dq1, w(1, 3))
    g = dot_cols(dq1, w(1, 4))
    taken = back = None
    for block in range(*SAME):
        dp, db2, db1 = edge_backward(block, g, 1)
        add_bias(4, 0.25 * db1)
        add_bias(5, 0.25 * db2)
        part = dot_plain(samehot[block - 5], dp.astype(BF16))
        taken = dp if taken is None else taken + dp
        back = part if back is None else back + part
    hsend[2] = back[:H].astype(BF16)
    hsend[3] = back[H + B:].astype(BF16)
    returns = [
        post(hsend.at[2], hback.at[1], place.beside(-1)),
        post(hsend.at[3], hback.at[0], place.beside(1)),
    ]
    own = back[H:H + B]
    layer2.advance()
    lifted = ext[H:H + B]
    taken_half = taken.astype(BF16)
    layer1.put(1, 1.0 * dot_rows(lifted, taken_half))
    layer1.put(2, dot_rows(act[5:11].reshape(6 * B, B), dys[5:11].reshape(6 * B, B)))
    layer1.put(3, dot_rows(lifted, dq1))
    layer1.put(4, dot_rows(node_in[1], dq1))
    layer1.put(5, dot_rows(nact[1], dz1))
    grad_lifted = pres[0] + dot_cols(taken_half, w(1, 1))
    for copy in returns:
        copy.wait_recv()
    own += dot_plain(onehot[5], hback[...].reshape(B, B))
    own_half = own.astype(BF16)
    grad_lifted += dot_cols(own_half, w(1, 0))
    lifted_cot[...] = grad_lifted * math.sqrt(total_fine)
    layer1.put(0, dot_rows(lifted, own_half))
    layer1.advance()
    layer2.advance()

    dz0, dq0 = node_backward(0, grad_lifted, 0.25)
    table[...] = dot_cols(dq0, w(0, 4)).astype(BF16)
    taken = back = None
    for block in range(*UP):
        dp, db2, db1 = edge_backward(block, dot_rows(onehot[block], table[...]), 0)
        add_bias(0, db1)
        add_bias(1, db2)
        part = dot_plain(onehot[block], dp.astype(BF16))
        taken = dp if taken is None else taken + dp
        back = part if back is None else back + part
    edge0.put(0, dot_rows(fine[...], taken.astype(BF16)))
    edge0.put(1, dot_rows(coarse[...], back.astype(BF16)))
    edge0.put(2, dot_rows(act[0:2].reshape(2 * B, B), dys[0:2].reshape(2 * B, B)))
    edge0.advance()
    bias_waits = [post(bias_acc, bias_core, place.partner())]
    node0.put(0, dot_rows(coarse[...], dq0))
    node0.put(1, dot_rows(node_in[0], dq0))
    node0.put(2, dot_rows(nact[0], dz0))
    node0.advance()

    def bias_step(step):
        for copy in bias_waits:
            copy.wait_recv()
        bias_waits.clear()
        if step == 0:
            total = bias_acc[...] + bias_core[...]
        else:
            total = bias_slots[step - 1, 0] + bias_slots[step - 1, 1]
            total = total + bias_slots[step - 1, 2] + bias_slots[step - 1, 3]
        if step == 3:
            gbias[...] = total
            return
        axis = "yxz"[step]
        at = place.at(axis)
        bias_slots[step, at] = total
        for d in (1, 2, 3):
            spot = bias_slots.at[step, at]
            bias_waits.append(post(spot, spot, place.peer(axis, d)))

    layer2.advance()
    layer1.advance()
    for step in range(7):
        edge0.advance()
        node0.advance()
        if layer2.step < 8:
            layer2.advance()
        if layer1.step < 8:
            layer1.advance()
        if step < 4:
            bias_step(step)
    assert all(group.step == 8 for group in (edge0, node0, layer1, layer2))
    for copy in posted:
        copy.wait_send()


def finish(fine_in, lifted_in, grads, gbias, fine_out, lifted_out, matrices_out, biases_out, wide, sems):
    copies = [
        pltpu.make_async_copy(fine_in, fine_out, sems.at[18]),
        pltpu.make_async_copy(lifted_in, lifted_out, sems.at[19]),
    ]
    for copy in copies:
        copy.start()
    for i in range(18):
        wide[i] = grads[i].astype(F32)
        copies.append(pltpu.make_async_copy(wide.at[i], matrices_out.at[i // 6, i % 6], sems.at[i]))
        copies[-1].start()
    for layer in range(3):
        biases_out[layer] = gbias[4 * layer:4 * layer + 4, :]
    for copy in copies:
        copy.wait()


def group_scratch(count):
    return [
        pltpu.VMEM((2, count, B, H), BF16),
        pltpu.VMEM((count, B, H), BF16),
        pltpu.VMEM((count, B, H), BF16),
        pltpu.VMEM((3, count, 64, H), BF16),
        pltpu.VMEM((count, 64, H), BF16),
        pltpu.VMEM((3, count, 16, H), BF16),
        pltpu.VMEM((count, 16, H), BF16),
        pltpu.VMEM((4, count, 16, H), BF16),
        pltpu.VMEM((count, 16, H), BF16),
    ]


def local(fine_state, coarse_state, up_target, down_source, halo_lists, same_source, matrices, biases, fine_cotangent):
    total_fine = fine_state.shape[0] * lax.axis_size("gx") * lax.axis_size("gy")
    scratch = [
        pltpu.SemaphoreType.DMA((COPIES,)),
        pltpu.SemaphoreType.DMA((COPIES,)),
        pltpu.VMEM((6, B, B), BF16),
        pltpu.VMEM((6, 2 * B, B), BF16),
        pltpu.VMEM((11, B, B), BF16),
        pltpu.VMEM((11, B, B), BF16),
        pltpu.VMEM((11, B, B), BF16),
        pltpu.VMEM((11, B, 1), F32),
        pltpu.VMEM((11, B, B), BF16),
        pltpu.VMEM((4, B, B), BF16),
        pltpu.VMEM((3, B, B), BF16),
        pltpu.VMEM((3, B, B), BF16),
        pltpu.VMEM((3, B, 1), F32),
        pltpu.VMEM((B, B), BF16),
        pltpu.VMEM((2 * B, B), BF16),
        pltpu.VMEM((2 * B, B), BF16),
        pltpu.VMEM((5, B, B), F32),
        pltpu.VMEM((4, 2, H, B), BF16),
        pltpu.VMEM((4, 2, H, B), BF16),
        pltpu.VMEM((4, H, B), BF16),
        pltpu.VMEM((2, H, B), BF16),
        pltpu.VMEM((3, B, B), BF16),
        pltpu.VMEM((16, B), F32),
        pltpu.VMEM((16, B), F32),
        pltpu.VMEM((3, 4, 16, B), F32),
        pltpu.VMEM((16, H), jnp.int32),
        pltpu.VMEM((16, B), jnp.int32),
    ]
    for count in (3, 3, 6, 6):
        scratch += group_scratch(count)
    vmem = pl.BlockSpec(memory_space=pltpu.VMEM)

    def body(*refs):
        kernel(total_fine, *refs)

    fine_out, lifted, grads, gbias = pl.pallas_call(
        body,
        out_shape=(
            jax.ShapeDtypeStruct((B, B), BF16),
            jax.ShapeDtypeStruct((B, B), F32),
            jax.ShapeDtypeStruct((18, B, B), BF16),
            jax.ShapeDtypeStruct((16, B), F32),
        ),
        in_specs=[vmem] * 9,
        out_specs=(vmem,) * 4,
        scratch_shapes=scratch,
        compiler_params=pltpu.CompilerParams(
            collective_id=0, has_side_effects=True, vmem_limit_bytes=32 << 20
        ),
        name="sweep",
    )(
        fine_state, coarse_state, fine_cotangent, up_target.reshape(4, H), down_source.reshape(6, H), halo_lists,
        same_source.reshape(12, H), matrices, biases,
    )
    hbm = pl.BlockSpec(memory_space=pl.ANY)
    return pl.pallas_call(
        finish,
        out_shape=(
            jax.ShapeDtypeStruct((B, B), BF16),
            jax.ShapeDtypeStruct((B, B), F32),
            jax.ShapeDtypeStruct((3, 6, B, B), F32),
            jax.ShapeDtypeStruct((3, 4, B), F32),
        ),
        in_specs=[vmem] * 4,
        out_specs=(hbm, hbm, hbm, vmem),
        scratch_shapes=[pltpu.VMEM((18, B, B), F32), pltpu.SemaphoreType.DMA((20,))],
        compiler_params=pltpu.CompilerParams(vmem_limit_bytes=16 << 20),
        name="finish",
    )(fine_out, lifted, grads, gbias)


def solution(mesh):
    in_specs = (
        P(("gx", "gy"), None),
        P("gy", None),
        P(("gx", "gy")),
        P(("gx", "gy")),
        P("gy", None),
        P("gy"),
        P(),
        P(),
        P(("gx", "gy"), None),
    )
    out_specs = (P(("gx", "gy"), None), P("gy", None), P(), P())
    return jax.shard_map(local, mesh=mesh, in_specs=in_specs, out_specs=out_specs, check_vma=False)
```

time: 428 us -> 86 us (0.20); the launches traced: 420 us -> 85.6 us
  waiting for transfers between devices: 147 us -> 0 us
  Pallas kernels: 0 us -> 77.2 us
  blocking collectives: 68.5 us -> 0 us
  local copies, waits for them, and re-layouts: 68.5 us -> 7.82 us
  matrix products: 57.8 us -> 0 us
  other arithmetic: 54 us -> 0 us
  between operations: 15.9 us -> 0.66 us
  starting transfers between devices: 8.44 us -> 0 us
    psum x3 -> x0, waiting for transfers between devices: 144 us -> none  [the longest x1 79.4 us: local(): lax.psum((local_matrices, local_biases), ('gx', 'gy'))]
    pallas_call x0 -> x2, Pallas kernels: none -> 77.2 us  [the longest x1 74.1 us: local(): pl.pallas_call(body, out_shape=(jax.ShapeDtypeStruct((B, B), BF16), jax.S...]
    psum x1 -> x0, blocking collectives: 68.5 us -> none  [local(): lax.psum((local_matrices, local_biases), ('gx', 'gy'))]
    dot_general x49 -> x0, matrix products: 57.8 us -> none  [the longest x18 23.9 us: dot_plain(): return jnp.dot(left_side, right_side, preferred_element_type=jnp.float32)]
    scatter-add x5 -> x0, other arithmetic: 22.1 us -> none  [the longest x1 9.04 us: local(): jax.ops.segment_sum(same_grad, same_source, num_segments=rows_coarse + 2...]
    gather x13 -> x0, local copies, waits for them, and re-layouts: 18.7 us -> none  [the longest x2 6.13 us: same_edges(): sent_rows[sources].reshape(node_count, -1, feature_width)]
    reduce_sum x26 -> x0, other arithmetic: 17.7 us -> none  [the longest x6 3.45 us: layer_norm(): centred = values - centre]
    unnamed x291 -> x18, local copies, waits for them, and re-layouts: 23.5 us -> 7.82 us
  transfers between devices with their start and end apart: 7 -> 0, of which waited for: 5 -> 0; matrix products, arithmetic and copies ran while one was open for 7% -> 0% of each run, Pallas kernels for 0% -> 0%
where the time goes in v1:
time: 86 us; the launch traced here: 85.6 us
  Pallas kernels  77.2 us (90%)
  local copies, waits for them, and re-layouts  7.82 us (9%)
    pallas_call x1, Pallas kernels, local(): pl.pallas_call(body, out_shape=(jax.ShapeDtypeStruct((B, B), BF16), jax.S...  74.1 us
    unnamed x18, local copies, waits for them, and re-layouts  7.82 us
    pallas_call x1, Pallas kernels, local(): pl.pallas_call(finish, out_shape=(jax.ShapeDtypeStruct((B, B), BF16), jax...  3.05 us

profile of v1, /device:TPU:1, one launch (start us, length us, event | category | flops | bytes accessed | tf_op | source)
XLA Modules:
  0.0 85.6 jit_solution(4182361801222513489)
XLA Ops:
  0.6 0.0 copy-start
  0.6 1.7 %copy-done = bf16[3,6,256,256]{3,2,1,0:T(8,128)(2,1)S(1)} copy-done((bf16[3,6,256,256]{3,2,1,0:T(8,128)(2,1)S(1)}, bf16[3,6,256,256]{3,2,1,0:T(8,128)(2,1)}, u32[]{:S(2)}) %copy-start) | copy-done | bytes 2359320
  2.3 0.0 copy-start.1
  2.3 0.9 %copy-done.1 = bf16[256,256]{1,0:T(8,128)(2,1)S(1)} copy-done((bf16[256,256]{1,0:T(8,128)(2,1)S(1)}, bf16[256,256]{1,0:T(8,128)(2,1)}, u32[]{:S(2)}) %copy-start.1) | copy-done | bytes 131096
  3.2 0.0 copy-start.2
  3.2 0.9 %copy-done.2 = bf16[256,256]{1,0:T(8,128)(2,1)S(1)} copy-done((bf16[256,256]{1,0:T(8,128)(2,1)S(1)}, bf16[256,256]{1,0:T(8,128)(2,1)}, u32[]{:S(2)}) %copy-start.2) | copy-done | bytes 131096
  4.1 0.0 copy-start.3
  4.1 0.9 %copy-done.3 = bf16[256,256]{1,0:T(8,128)(2,1)S(1)} copy-done((bf16[256,256]{1,0:T(8,128)(2,1)S(1)}, bf16[256,256]{1,0:T(8,128)(2,1)}, u32[]{:S(2)}) %copy-start.3) | copy-done | bytes 131096
  5.0 0.0 copy-start.4
  5.0 0.7 copy-done.4
  5.7 0.0 copy-start.5
  5.7 0.7 copy-done.5
  6.4 0.0 copy-start.6
  6.4 0.7 copy-done.6
  7.1 0.0 copy-start.7
  7.1 0.7 copy-done.7
  7.8 0.0 copy-start.8
  7.8 0.7 copy-done.8
  8.5 74.1 %sweep.1 = (bf16[256,256]{1,0:T(8,128)(2,1)S(1)}, f32[256,256]{1,0:T(8,128)S(1)}, bf16[18,256,256]{2,1,0:T(8,128)(2,1)S(1)}, f32[16,256]{1,0:T(8,128)S(1)}) custom-call(bf16[256,256]{1,0:T(8,128)(2,1)S(1)} %copy-done.1, bf16[256,256]{1,0:T(8,128)(2,1)S(1)} %copy-done.2, bf16[256,256]{1,0:T(8,128)(2,1)S(1)} %copy-done.3, s32[4,128]{1,0:T(4,128)S(1)} %bitcast.5, ...), custom_call_target="tpu_custom_call" | custom-call | tf_op jit(solution)/shard_map/sweep/pallas_call | solution.py:549
  82.6 3.1 %finish.1 = (bf16[256,256]{1,0:T(8,128)(2,1)}, f32[256,256]{1,0:T(8,128)}, f32[3,6,256,256]{3,2,1,0:T(8,128)}, f32[3,4,256]{2,1,0:T(4,128)}) custom-call(bf16[256,256]{1,0:T(8,128)(2,1)S(1)} %get-tuple-element.8.fine_in, f32[256,256]{1,0:T(8,128)S(1)} %get-tuple-element.9.lifted_in, bf16[18,256,256]{2,1,0:T(8,128)(2,1)S(1)} %get-tuple-element.10.grads, ...), custom_call_target="tpu_custom_call" | custom-call | tf_op jit(solution)/shard_map/finish/pallas_call | solution.py:569
Async XLA Ops:
  0.6 1.7 %copy-start = (bf16[3,6,256,256]{3,2,1,0:T(8,128)(2,1)S(1)}, bf16[3,6,256,256]{3,2,1,0:T(8,128)(2,1)}, u32[]{:S(2)}) copy-start(bf16[3,6,256,256]{3,2,1,0:T(8,128)(2,1)} %refs_7_.1) | copy-start | bytes 7077892
  2.3 0.9 %copy-start.1 = (bf16[256,256]{1,0:T(8,128)(2,1)S(1)}, bf16[256,256]{1,0:T(8,128)(2,1)}, u32[]{:S(2)}) copy-start(bf16[256,256]{1,0:T(8,128)(2,1)} %refs_0_.1) | copy-start | bytes 393220
  3.2 0.9 %copy-start.2 = (bf16[256,256]{1,0:T(8,128)(2,1)S(1)}, bf16[256,256]{1,0:T(8,128)(2,1)}, u32[]{:S(2)}) copy-start(bf16[256,256]{1,0:T(8,128)(2,1)} %refs_1_.1) | copy-start | bytes 393220
  4.1 0.9 %copy-start.3 = (bf16[256,256]{1,0:T(8,128)(2,1)S(1)}, bf16[256,256]{1,0:T(8,128)(2,1)}, u32[]{:S(2)}) copy-start(bf16[256,256]{1,0:T(8,128)(2,1)} %refs_2_.1) | copy-start | bytes 393220
  5.0 0.7 copy-start.4
  5.7 0.7 copy-start.5
  6.4 0.7 copy-start.6
  7.1 0.7 copy-start.7
  7.8 0.7 copy-start.8

commit v2 on v1

--- a/solution.py
+++ b/solution.py
@@ -193,10 +193,11 @@
 
 
 def kernel(total_fine, *refs):
-    (fine, coarse, cot, up_raw, down_raw, halo_raw, same_raw, mats, bias, fine_out, lifted_cot, grads, gbias) = refs[:13]
+    inputs, (fine_out, lifted_cot, grads, gbias) = refs[:9], refs[9:13]
     (send_sems, recv_sems, onehot, samehot, act, slope, unit, scale, dys, nact, nslope, nunit, nscale,
-     table, ext, gtab, pres, csend, crecv, hsend, hback, node_in, bias_acc, bias_core, bias_slots, raw, index) = refs[13:40]
-    group_refs = refs[40:]
+     table, ext, gtab, pres, csend, crecv, hsend, hback, node_in, bias_acc, bias_core, bias_slots, raw, index, load_sems,
+     fine, coarse, cot, up_raw, down_raw, halo_raw, same_raw, mats, bias) = refs[13:50]
+    group_refs = refs[50:]
     place = Place()
     posted = []
 
@@ -216,6 +217,16 @@
     for device in near:
         pl.semaphore_signal(barrier, inc=1, device_id=device, device_id_type=MESH)
 
+    loads = []
+    for i, (src, dst) in enumerate([
+        (inputs[3], up_raw), (inputs[0], fine), (inputs[1], coarse), (inputs[8], bias),
+        (inputs[7].at[0, 0:3], mats.at[0, 0:3]), (inputs[4], down_raw), (inputs[6], same_raw), (inputs[5], halo_raw),
+        (inputs[7].at[0, 3:6], mats.at[0, 3:6]), (inputs[7].at[2], mats.at[2]), (inputs[7].at[1], mats.at[1]),
+        (inputs[2], cot),
+    ]):
+        loads.append(pltpu.make_async_copy(src, dst, load_sems.at[i]))
+        loads[-1].start()
+
     def groups_of(at, axes, rows):
         return Group(post, place, axes, rows, group_refs[9 * at:9 * at + 9], grads)
 
@@ -225,6 +236,8 @@
     layer2 = groups_of(3, ("x", "z", "y"), slice(12, 18))
 
     bias_acc[...] = jnp.zeros_like(bias_acc)
+    for load in loads[:5]:
+        load.wait()
     deal(up_raw, raw, index, *UP)
 
     def add_bias(row, value):
@@ -321,6 +334,8 @@
 
     pl.semaphore_wait(barrier, len(near))
     state = sum_start(0, up_sum)
+    for load in loads[5:]:
+        load.wait()
     pres[0] = dot_plain(coarse[...], w(0, 3)) + b(0, 2)
     deal(down_raw, raw, index, *DOWN)
     deal(same_raw, raw, index, *SAME)
@@ -538,6 +553,16 @@
         pltpu.VMEM((3, 4, 16, B), F32),
         pltpu.VMEM((16, H), jnp.int32),
         pltpu.VMEM((16, B), jnp.int32),
+        pltpu.SemaphoreType.DMA((12,)),
+        pltpu.VMEM((B, B), BF16),
+        pltpu.VMEM((B, B), BF16),
+        pltpu.VMEM((B, B), BF16),
+        pltpu.VMEM((4, H), jnp.int32),
+        pltpu.VMEM((6, H), jnp.int32),
+        pltpu.VMEM((2, H), jnp.int32),
+        pltpu.VMEM((12, H), jnp.int32),
+        pltpu.VMEM((3, 6, B, B), BF16),
+        pltpu.VMEM((3, 4, B), F32),
     ]
     for count in (3, 3, 6, 6):
         scratch += group_scratch(count)
@@ -554,17 +579,20 @@
             jax.ShapeDtypeStruct((18, B, B), BF16),
             jax.ShapeDtypeStruct((16, B), F32),
         ),
-        in_specs=[vmem] * 9,
+        in_specs=[pl.BlockSpec(memory_space=pltpu.HBM)] * 9,
         out_specs=(vmem,) * 4,
         scratch_shapes=scratch,
         compiler_params=pltpu.CompilerParams(
             collective_id=0, has_side_effects=True, vmem_limit_bytes=32 << 20
         ),
         name="sweep",
-    )(
-        fine_state, coarse_state, fine_cotangent, up_target.reshape(4, H), down_source.reshape(6, H), halo_lists,
-        same_source.reshape(12, H), matrices, biases,
-    )
+    )(*[
+        pltpu.with_memory_space_constraint(value, pltpu.HBM)
+        for value in (
+            fine_state, coarse_state, fine_cotangent, up_target.reshape(4, H), down_source.reshape(6, H), halo_lists,
+            same_source.reshape(12, H), matrices, biases,
+        )
+    ])
     hbm = pl.BlockSpec(memory_space=pl.ANY)
     return pl.pallas_call(
         finish,

time: 86 us -> 77.7 us (0.903)
  local copies, waits for them, and re-layouts: 7.82 us -> 0 us
    unnamed x18 -> x0, local copies, waits for them, and re-layouts: 7.82 us -> none
where the time goes in v2:
time: 77.7 us; the launch traced here: 77.6 us
  Pallas kernels  76.9 us (99%)
    pallas_call x1, Pallas kernels, local(): pl.pallas_call(body, out_shape=(jax.ShapeDtypeStruct((B, B), BF16), jax.S...  73.9 us
    pallas_call x1, Pallas kernels, local(): pl.pallas_call(finish, out_shape=(jax.ShapeDtypeStruct((B, B), BF16), jax...  3.05 us

profile of v2, /device:TPU:1, one launch (start us, length us, event | category | flops | bytes accessed | tf_op | source)
XLA Modules:
  0.0 77.6 jit_solution(5859074531977140193)
XLA Ops:
  0.6 73.9 %sweep.1 = (bf16[256,256]{1,0:T(8,128)(2,1)S(1)}, f32[256,256]{1,0:T(8,128)S(1)}, bf16[18,256,256]{2,1,0:T(8,128)(2,1)S(1)}, f32[16,256]{1,0:T(8,128)S(1)}) custom-call(bf16[256,256]{1,0:T(8,128)(2,1)} %refs_0_.1, bf16[256,256]{1,0:T(8,128)(2,1)} %refs_1_.1, bf16[256,256]{1,0:T(8,128)(2,1)} %refs_2_.1, s32[4,128]{1,0:T(4,128)} %bitcast.5, s32[6,128]{1,0:T(8,128)} %bitcast.4, ...), custom_call_target="tpu_custom_call" | custom-call | tf_op jit(solution)/shard_map/sweep/pallas_call | solution.py:574
  74.5 3.1 %finish.1 = (bf16[256,256]{1,0:T(8,128)(2,1)}, f32[256,256]{1,0:T(8,128)}, f32[3,6,256,256]{3,2,1,0:T(8,128)}, f32[3,4,256]{2,1,0:T(4,128)}) custom-call(bf16[256,256]{1,0:T(8,128)(2,1)S(1)} %get-tuple-element.8.fine_in, f32[256,256]{1,0:T(8,128)S(1)} %get-tuple-element.9.lifted_in, bf16[18,256,256]{2,1,0:T(8,128)(2,1)S(1)} %get-tuple-element.10.grads, ...), custom_call_target="tpu_custom_call" | custom-call | tf_op jit(solution)/shard_map/finish/pallas_call | solution.py:597

commit v3 on v2

--- a/solution.py
+++ b/solution.py
@@ -13,7 +13,15 @@
 B = 256
 H = 128
 UP, DOWN, SAME = (0, 2), (2, 5), (5, 11)
-COPIES = 104
+COPIES = 120
+GROUPS = (
+    (("x", "z", "y"), 0, 2, False),
+    (("z", "x", "y"), 2, 3, False),
+    (("y", "x", "z"), 3, 6, True),
+    (("y", "z", "x"), 6, 12, True),
+    (("x", "z", "y"), 12, 15, False),
+    (("z", "x", "y"), 15, 18, False),
+)
 
 
 def dot_plain(a, b):
@@ -53,7 +61,8 @@
 
 
 class Group:
-    def __init__(self, post, place, axes, rows, refs, out):
+    def __init__(self, post, place, axes, rows, shared, refs, out):
+        self.shared = shared
         self.post, self.place, self.axes, self.rows, self.out = post, place, axes, rows, out
         self.g, self.rc, self.s1, self.r1, self.s2, self.r2, self.s3, self.r3, self.s4 = refs
         self.count = rows.stop - rows.start
@@ -76,13 +85,24 @@
         getattr(self, "step%d" % self.step)()
         self.step += 1
 
+    def quarter(self):
+        return pl.ds(pl.multiple_of(self.place.at(self.axes[0]) * 64, 64), 64)
+
     def step0(self):
         other = 1 - self.place.core
-        self.copies = [self.post(self.g.at[other], self.rc, self.place.partner())]
+        src = self.g.at[other, :, self.quarter(), :] if self.shared else self.g.at[other]
+        self.copies = [self.post(src, self.rc, self.place.partner())]
 
     def step1(self):
         self.landed()
         core = self.place.core
+        if self.shared:
+            for i in range(self.count):
+                own = self.g[core, i, self.quarter(), :].astype(F32)
+                self.s2[i] = (own + self.rc[i].astype(F32)).astype(BF16)
+            self.scatter(self.axes[1], 16, self.s2, self.r2)
+            self.step = 2
+            return
         for i in range(self.count):
             self.s1[i] = (self.g[core, i].astype(F32) + self.rc[i].astype(F32)).astype(BF16)
         self.scatter(self.axes[0], 64, self.s1, self.r1)
@@ -110,9 +130,6 @@
 
     def step3(self):
         self.landed()
-        if len(self.axes) == 2:
-            self.gather_sum(self.axes[1], 16, self.s2, self.r2, self.s4)
-            return
         self.gather_sum(self.axes[1], 16, self.s2, self.r2, self.s3)
         at = self.place.at(self.axes[2])
         for d in (1, 2, 3):
@@ -121,12 +138,11 @@
 
     def step4(self):
         self.landed()
-        if len(self.axes) == 3:
-            for i in range(self.count):
-                total = self.r3[0, i].astype(F32)
-                for j in (1, 2, 3):
-                    total += self.r3[j, i].astype(F32)
-                self.s4[i] = total.astype(BF16)
+        for i in range(self.count):
+            total = self.r3[0, i].astype(F32)
+            for j in (1, 2, 3):
+                total += self.r3[j, i].astype(F32)
+            self.s4[i] = total.astype(BF16)
         start = self.place.at(self.axes[0]) * 64 + self.place.at(self.axes[1]) * 16
         rows = pl.ds(pl.multiple_of(start, 16), 16)
         spot = self.out.at[self.rows, rows, self.lanes]
@@ -137,8 +153,7 @@
 
     def step5(self):
         self.landed()
-        rows = pl.ds(pl.multiple_of(self.place.at(self.axes[0]) * 64, 64), 64)
-        spot = self.out.at[self.rows, rows, self.lanes]
+        spot = self.out.at[self.rows, self.quarter(), self.lanes]
         for d in (1, 2, 3):
             self.copies.append(self.post(spot, spot, self.place.peer(self.axes[0], d)))
 
@@ -227,18 +242,20 @@
         loads.append(pltpu.make_async_copy(src, dst, load_sems.at[i]))
         loads[-1].start()
 
-    def groups_of(at, axes, rows):
-        return Group(post, place, axes, rows, group_refs[9 * at:9 * at + 9], grads)
-
-    edge0 = groups_of(0, ("y", "z", "x"), slice(0, 3))
-    node0 = groups_of(1, ("x", "z"), slice(3, 6))
-    layer1 = groups_of(2, ("z", "x"), slice(6, 12))
-    layer2 = groups_of(3, ("x", "z", "y"), slice(12, 18))
+    edge0a, edge0b, node0, layer1, layer2a, layer2b = [
+        Group(post, place, axes, slice(first, end), shared, group_refs[9 * at:9 * at + 9], grads)
+        for at, (axes, first, end, shared) in enumerate(GROUPS)
+    ]
 
     bias_acc[...] = jnp.zeros_like(bias_acc)
     for load in loads[:5]:
         load.wait()
     deal(up_raw, raw, index, *UP)
+
+    def step_on(*groups):
+        for group in groups:
+            if group.step < 8:
+                group.advance()
 
     def add_bias(row, value):
         bias_acc[row:row + 1, :] += value
@@ -389,16 +406,16 @@
         taken = dp if taken is None else taken + dp
         back = part if back is None else back + part
     state = sum_start(2, back)
-    layer2.put(1, dot_rows(fine[...], taken.astype(BF16)))
-    layer2.put(2, dot_rows(act[2:5].reshape(3 * B, B), dys[2:5].reshape(3 * B, B)))
+    layer2a.put(1, dot_rows(fine[...], taken.astype(BF16)))
+    layer2a.put(2, dot_rows(act[2:5].reshape(3 * B, B), dys[2:5].reshape(3 * B, B)))
     state = sum_middle(2, state)
-    layer2.put(3, dot_rows(fine[...], dq2))
-    layer2.put(4, dot_rows(node_in[2], dq2))
-    layer2.put(5, dot_rows(nact[2], dz2))
+    layer2b.put(0, dot_rows(fine[...], dq2))
+    layer2b.put(1, dot_rows(node_in[2], dq2))
+    layer2b.put(2, dot_rows(nact[2], dz2))
     sent_half = sum_end(2, state)
     grad_mixed = dot_cols(sent_half, w(2, 0))
-    layer2.put(0, 0.25 * dot_rows(nact[3], sent_half))
-    layer2.advance()
+    layer2a.put(0, 0.25 * dot_rows(nact[3], sent_half))
+    step_on(layer2a, layer2b)
 
     dz1, dq1 = node_backward(1, grad_mixed, 0.25)
     pres[0] = grad_mixed + dot_cols(dq1, w(1, 3))
@@ -418,7 +435,7 @@
         post(hsend.at[3], hback.at[0], place.beside(1)),
     ]
     own = back[H:H + B]
-    layer2.advance()
+    step_on(layer2a, layer2b)
     lifted = ext[H:H + B]
     taken_half = taken.astype(BF16)
     layer1.put(1, 1.0 * dot_rows(lifted, taken_half))
@@ -427,6 +444,7 @@
     layer1.put(4, dot_rows(node_in[1], dq1))
     layer1.put(5, dot_rows(nact[1], dz1))
     grad_lifted = pres[0] + dot_cols(taken_half, w(1, 1))
+    step_on(layer2a, layer2b)
     for copy in returns:
         copy.wait_recv()
     own += dot_plain(onehot[5], hback[...].reshape(B, B))
@@ -434,11 +452,11 @@
     grad_lifted += dot_cols(own_half, w(1, 0))
     lifted_cot[...] = grad_lifted * math.sqrt(total_fine)
     layer1.put(0, dot_rows(lifted, own_half))
-    layer1.advance()
-    layer2.advance()
+    step_on(layer1)
 
     dz0, dq0 = node_backward(0, grad_lifted, 0.25)
     table[...] = dot_cols(dq0, w(0, 4)).astype(BF16)
+    step_on(layer2a, layer2b, layer1)
     taken = back = None
     for block in range(*UP):
         dp, db2, db1 = edge_backward(block, dot_rows(onehot[block], table[...]), 0)
@@ -447,15 +465,15 @@
         part = dot_plain(onehot[block], dp.astype(BF16))
         taken = dp if taken is None else taken + dp
         back = part if back is None else back + part
-    edge0.put(0, dot_rows(fine[...], taken.astype(BF16)))
-    edge0.put(1, dot_rows(coarse[...], back.astype(BF16)))
-    edge0.put(2, dot_rows(act[0:2].reshape(2 * B, B), dys[0:2].reshape(2 * B, B)))
-    edge0.advance()
+    edge0a.put(0, dot_rows(fine[...], taken.astype(BF16)))
+    edge0a.put(1, dot_rows(coarse[...], back.astype(BF16)))
+    edge0b.put(0, dot_rows(act[0:2].reshape(2 * B, B), dys[0:2].reshape(2 * B, B)))
+    step_on(edge0a, edge0b)
     bias_waits = [post(bias_acc, bias_core, place.partner())]
     node0.put(0, dot_rows(coarse[...], dq0))
     node0.put(1, dot_rows(node_in[0], dq0))
     node0.put(2, dot_rows(nact[0], dz0))
-    node0.advance()
+    step_on(node0)
 
     def bias_step(step):
         for copy in bias_waits:
@@ -476,18 +494,11 @@
             spot = bias_slots.at[step, at]
             bias_waits.append(post(spot, spot, place.peer(axis, d)))
 
-    layer2.advance()
-    layer1.advance()
     for step in range(7):
-        edge0.advance()
-        node0.advance()
-        if layer2.step < 8:
-            layer2.advance()
-        if layer1.step < 8:
-            layer1.advance()
+        step_on(edge0a, edge0b, node0, layer2a, layer2b, layer1)
         if step < 4:
             bias_step(step)
-    assert all(group.step == 8 for group in (edge0, node0, layer1, layer2))
+    assert all(group.step == 8 for group in (edge0a, edge0b, node0, layer1, layer2a, layer2b))
     for copy in posted:
         copy.wait_send()
 
@@ -509,12 +520,14 @@
         copy.wait()
 
 
-def group_scratch(count):
+def group_scratch(count, shared):
+    whole = 64 if shared else B
+    spare = 16 if shared else B
     return [
         pltpu.VMEM((2, count, B, H), BF16),
-        pltpu.VMEM((count, B, H), BF16),
-        pltpu.VMEM((count, B, H), BF16),
-        pltpu.VMEM((3, count, 64, H), BF16),
+        pltpu.VMEM((count, whole, H), BF16),
+        pltpu.VMEM((count, spare, H), BF16),
+        pltpu.VMEM((3, count, spare // 4, H), BF16),
         pltpu.VMEM((count, 64, H), BF16),
         pltpu.VMEM((3, count, 16, H), BF16),
         pltpu.VMEM((count, 16, H), BF16),
@@ -564,8 +577,8 @@
         pltpu.VMEM((3, 6, B, B), BF16),
         pltpu.VMEM((3, 4, B), F32),
     ]
-    for count in (3, 3, 6, 6):
-        scratch += group_scratch(count)
+    for _, first, end, shared in GROUPS:
+        scratch += group_scratch(end - first, shared)
     vmem = pl.BlockSpec(memory_space=pltpu.VMEM)
 
     def body(*refs):

time: 77.7 us -> 75.8 us (0.976)
  Pallas kernels: 76.9 us -> 75 us
    pallas_call x1, Pallas kernels: 73.9 us -> 71.9 us  [local(): pl.pallas_call(body, out_shape=(jax.ShapeDtypeStruct((B, B), BF16), jax.S...]
where the time goes in v3:
time: 75.8 us; the launch traced here: 75.6 us
  Pallas kernels  75 us (99%)
    pallas_call x1, Pallas kernels, local(): pl.pallas_call(body, out_shape=(jax.ShapeDtypeStruct((B, B), BF16), jax.S...  71.9 us
    pallas_call x1, Pallas kernels, local(): pl.pallas_call(finish, out_shape=(jax.ShapeDtypeStruct((B, B), BF16), jax...  3.05 us

profile of v3, /device:TPU:1, one launch (start us, length us, event | category | flops | bytes accessed | tf_op | source)
XLA Modules:
  0.0 75.6 jit_solution(10204333564340059897)
XLA Ops:
  0.6 71.9 %sweep.1 = (bf16[256,256]{1,0:T(8,128)(2,1)S(1)}, f32[256,256]{1,0:T(8,128)S(1)}, bf16[18,256,256]{2,1,0:T(8,128)(2,1)S(1)}, f32[16,256]{1,0:T(8,128)S(1)}) custom-call(bf16[256,256]{1,0:T(8,128)(2,1)} %refs_0_.1, bf16[256,256]{1,0:T(8,128)(2,1)} %refs_1_.1, bf16[256,256]{1,0:T(8,128)(2,1)} %refs_2_.1, s32[4,128]{1,0:T(4,128)} %bitcast.5, s32[6,128]{1,0:T(8,128)} %bitcast.4, ...), custom_call_target="tpu_custom_call" | custom-call | tf_op jit(solution)/shard_map/sweep/pallas_call | solution.py:587
  72.6 3.1 %finish.1 = (bf16[256,256]{1,0:T(8,128)(2,1)}, f32[256,256]{1,0:T(8,128)}, f32[3,6,256,256]{3,2,1,0:T(8,128)}, f32[3,4,256]{2,1,0:T(4,128)}) custom-call(bf16[256,256]{1,0:T(8,128)(2,1)S(1)} %get-tuple-element.8.fine_in, f32[256,256]{1,0:T(8,128)S(1)} %get-tuple-element.9.lifted_in, bf16[18,256,256]{2,1,0:T(8,128)(2,1)S(1)} %get-tuple-element.10.grads, ...), custom_call_target="tpu_custom_call" | custom-call | tf_op jit(solution)/shard_map/finish/pallas_call | solution.py:610

commit v4 on v3

--- a/solution.py
+++ b/solution.py
@@ -13,14 +13,16 @@
 B = 256
 H = 128
 UP, DOWN, SAME = (0, 2), (2, 5), (5, 11)
-COPIES = 120
+COPIES = 160
+PIECES = 4
 GROUPS = (
-    (("x", "z", "y"), 0, 2, False),
-    (("z", "x", "y"), 2, 3, False),
-    (("y", "x", "z"), 3, 6, True),
-    (("y", "z", "x"), 6, 12, True),
-    (("x", "z", "y"), 12, 15, False),
-    (("z", "x", "y"), 15, 18, False),
+    ("quick", ("x", "y", "z"), 0, 1),
+    ("quick", ("z", "x", "y"), 1, 2),
+    ("quick", ("y", "z", "x"), 2, 3),
+    ("same", ("y", "x", "z"), 3, 6),
+    ("same", ("y", "z", "x"), 6, 12),
+    ("fine", ("x", "z", "y"), 12, 15),
+    ("fine", ("z", "x", "y"), 15, 18),
 )
 
 
@@ -67,9 +69,7 @@
         self.g, self.rc, self.s1, self.r1, self.s2, self.r2, self.s3, self.r3, self.s4 = refs
         self.count = rows.stop - rows.start
         self.step = 0
-        core = place.core
         self.copies = []
-        self.lanes = pl.ds(pl.multiple_of(core * H, H), H)
 
     def put(self, i, value):
         half = value.astype(BF16)
@@ -131,39 +131,67 @@
     def step3(self):
         self.landed()
         self.gather_sum(self.axes[1], 16, self.s2, self.r2, self.s3)
-        at = self.place.at(self.axes[2])
+        self.share(self.axes[2], self.s3, self.r3)
+
+    def share(self, axis, src, slots):
+        at = self.place.at(axis)
         for d in (1, 2, 3):
-            self.copies.append(self.post(self.s3, self.r3.at[at], self.place.peer(self.axes[2], d)))
-        self.r3[at] = self.s3[...]
+            self.copies.append(self.post(src, slots.at[at], self.place.peer(axis, d)))
+        slots[at] = src[...]
+
+    def slot_sum(self, slots, out):
+        for i in range(self.count):
+            total = slots[0, i].astype(F32)
+            for j in (1, 2, 3):
+                total += slots[j, i].astype(F32)
+            out[i] = total.astype(BF16)
 
     def step4(self):
         self.landed()
-        for i in range(self.count):
-            total = self.r3[0, i].astype(F32)
-            for j in (1, 2, 3):
-                total += self.r3[j, i].astype(F32)
-            self.s4[i] = total.astype(BF16)
+        self.slot_sum(self.r3, self.s4)
         start = self.place.at(self.axes[0]) * 64 + self.place.at(self.axes[1]) * 16
         rows = pl.ds(pl.multiple_of(start, 16), 16)
-        spot = self.out.at[self.rows, rows, self.lanes]
+        spot = self.out.at[self.place.core, self.rows, rows, :]
         for d in (1, 2, 3):
             self.copies.append(self.post(self.s4, spot, self.place.peer(self.axes[1], d)))
         for i in range(self.count):
-            self.out[self.rows.start + i, rows, self.lanes] = self.s4[i]
+            self.out[self.place.core, self.rows.start + i, rows, :] = self.s4[i]
 
     def step5(self):
         self.landed()
-        spot = self.out.at[self.rows, self.quarter(), self.lanes]
+        spot = self.out.at[self.place.core, self.rows, self.quarter(), :]
         for d in (1, 2, 3):
             self.copies.append(self.post(spot, spot, self.place.peer(self.axes[0], d)))
 
     def step6(self):
         self.landed()
-        spot = self.out.at[self.rows, :, self.lanes]
+        spot = self.out.at[self.place.core, self.rows, :, :]
         self.copies = [self.post(spot, spot, self.place.partner())]
 
     def step7(self):
         self.landed()
+
+
+class Quick(Group):
+    def step2(self):
+        self.landed()
+        self.gather_sum(self.axes[0], 64, self.s1, self.r1, self.s2)
+        self.share(self.axes[1], self.s2, self.r2)
+
+    def step3(self):
+        self.landed()
+        self.slot_sum(self.r2, self.s3)
+        self.share(self.axes[2], self.s3, self.r3)
+
+    def step4(self):
+        self.landed()
+        self.slot_sum(self.r3, self.s4)
+        spot = self.out.at[self.place.core, self.rows, self.quarter(), :]
+        for d in (1, 2, 3):
+            self.copies.append(self.post(self.s4, spot, self.place.peer(self.axes[0], d)))
+        for i in range(self.count):
+            self.out[self.place.core, self.rows.start + i, self.quarter(), :] = self.s4[i]
+        self.step = 5
 
 
 class Place:
@@ -210,9 +238,9 @@
 def kernel(total_fine, *refs):
     inputs, (fine_out, lifted_cot, grads, gbias) = refs[:9], refs[9:13]
     (send_sems, recv_sems, onehot, samehot, act, slope, unit, scale, dys, nact, nslope, nunit, nscale,
-     table, ext, gtab, pres, csend, crecv, hsend, hback, node_in, bias_acc, bias_core, bias_slots, raw, index, load_sems,
-     fine, coarse, cot, up_raw, down_raw, halo_raw, same_raw, mats, bias) = refs[13:50]
-    group_refs = refs[50:]
+     table, ext, gtab, pres, csend, crecv, hsend, hback, node_in, bias_acc, bias_core, bias_slots, raw, index, load_sems, summed,
+     fine, coarse, cot, up_raw, down_raw, halo_raw, same_raw, mats, bias) = refs[13:51]
+    group_refs = refs[51:]
     place = Place()
     posted = []
 
@@ -242,10 +270,13 @@
         loads.append(pltpu.make_async_copy(src, dst, load_sems.at[i]))
         loads[-1].start()
 
-    edge0a, edge0b, node0, layer1, layer2a, layer2b = [
-        Group(post, place, axes, slice(first, end), shared, group_refs[9 * at:9 * at + 9], grads)
-        for at, (axes, first, end, shared) in enumerate(GROUPS)
+    groups = [
+        (Quick if kind == "quick" else Group)(
+            post, place, axes, slice(first, end), kind == "same", group_refs[9 * at:9 * at + 9], grads
+        )
+        for at, (kind, axes, first, end) in enumerate(GROUPS)
     ]
+    edge0, (node0, layer1, layer2a, layer2b) = groups[:3], groups[3:]
 
     bias_acc[...] = jnp.zeros_like(bias_acc)
     for load in loads[:5]:
@@ -307,6 +338,9 @@
         add_bias(4 * layer + 2, share * col_sum(dq))
         return dz16, dq16
 
+    def piece(i):
+        return pl.ds(i * (H // PIECES), H // PIECES)
+
     def sum_start(first, value):
         half = value.astype(BF16)
         csend[first, 0] = half[:H]
@@ -314,30 +348,34 @@
         odd = lax.rem(place.gx, 2)
         one = (place.gx + 1 - 2 * odd, place.gy)
         two = (lax.rem(place.gx + 2 * odd + 3, 4), place.gy)
-        waits = [
-            post(csend.at[first, 0], crecv.at[first, 0], one),
-            post(csend.at[first, 1], crecv.at[first, 1], two),
-        ]
+        waits = []
+        for i in range(PIECES):
+            for side, device in ((0, one), (1, two)):
+                waits.append(post(csend.at[first, side, piece(i)], crecv.at[first, side, piece(i)], device))
         return waits, one, two
+
+    def sum_pieces(at, waits, out, then):
+        for i in range(PIECES):
+            for side in (0, 1):
+                waits[2 * i + side].wait_recv()
+                both = csend[at, side, piece(i)].astype(F32) + crecv[at, side, piece(i)].astype(F32)
+                out[side, piece(i)] = both.astype(BF16)
+                then(i, side)
 
     def sum_middle(first, state):
         waits, one, two = state
-        for i in (0, 1):
-            waits[i].wait_recv()
-            both = csend[first, i].astype(F32) + crecv[first, i].astype(F32)
-            csend[first + 1, i] = both.astype(BF16)
-        return [
-            post(csend.at[first + 1, 0], crecv.at[first + 1, 0], two),
-            post(csend.at[first + 1, 1], crecv.at[first + 1, 1], one),
-        ]
+        later = []
+
+        def send_on(i, side):
+            device = (two, one)[side]
+            later.append(post(csend.at[first + 1, side, piece(i)], crecv.at[first + 1, side, piece(i)], device))
+
+        sum_pieces(first, waits, csend.at[first + 1], send_on)
+        return later
 
     def sum_end(first, waits):
-        parts = []
-        for i in (0, 1):
-            waits[i].wait_recv()
-            both = csend[first + 1, i].astype(F32) + crecv[first + 1, i].astype(F32)
-            parts.append(both.astype(BF16))
-        return jnp.concatenate(parts, axis=0)
+        sum_pieces(first + 1, waits, summed, lambda i, side: None)
+        return summed[...].reshape(B, B)
 
     for block in range(*UP):
         onehot[block] = hot_rows(block, B)
@@ -444,7 +482,6 @@
     layer1.put(4, dot_rows(node_in[1], dq1))
     layer1.put(5, dot_rows(nact[1], dz1))
     grad_lifted = pres[0] + dot_cols(taken_half, w(1, 1))
-    step_on(layer2a, layer2b)
     for copy in returns:
         copy.wait_recv()
     own += dot_plain(onehot[5], hback[...].reshape(B, B))
@@ -456,7 +493,7 @@
 
     dz0, dq0 = node_backward(0, grad_lifted, 0.25)
     table[...] = dot_cols(dq0, w(0, 4)).astype(BF16)
-    step_on(layer2a, layer2b, layer1)
+    step_on(layer2a, layer2b)
     taken = back = None
     for block in range(*UP):
         dp, db2, db1 = edge_backward(block, dot_rows(onehot[block], table[...]), 0)
@@ -465,10 +502,10 @@
         part = dot_plain(onehot[block], dp.astype(BF16))
         taken = dp if taken is None else taken + dp
         back = part if back is None else back + part
-    edge0a.put(0, dot_rows(fine[...], taken.astype(BF16)))
-    edge0a.put(1, dot_rows(coarse[...], back.astype(BF16)))
-    edge0b.put(0, dot_rows(act[0:2].reshape(2 * B, B), dys[0:2].reshape(2 * B, B)))
-    step_on(edge0a, edge0b)
+    edge0[0].put(0, dot_rows(fine[...], taken.astype(BF16)))
+    edge0[1].put(0, dot_rows(coarse[...], back.astype(BF16)))
+    edge0[2].put(0, dot_rows(act[0:2].reshape(2 * B, B), dys[0:2].reshape(2 * B, B)))
+    step_on(*edge0)
     bias_waits = [post(bias_acc, bias_core, place.partner())]
     node0.put(0, dot_rows(coarse[...], dq0))
     node0.put(1, dot_rows(node_in[0], dq0))
@@ -494,11 +531,12 @@
             spot = bias_slots.at[step, at]
             bias_waits.append(post(spot, spot, place.peer(axis, d)))
 
-    for step in range(7):
-        step_on(edge0a, edge0b, node0, layer2a, layer2b, layer1)
+    for step in range(6):
+        step_on(*edge0, node0, layer1, layer2a, layer2b)
         if step < 4:
             bias_step(step)
-    assert all(group.step == 8 for group in (edge0a, edge0b, node0, layer1, layer2a, layer2b))
+    assert all(group.step == 8 for group in groups)
+    assert len(posted) <= COPIES
     for copy in posted:
         copy.wait_send()
 
@@ -511,7 +549,8 @@
     for copy in copies:
         copy.start()
     for i in range(18):
-        wide[i] = grads[i].astype(F32)
+        wide[i, :, :H] = grads[0, i].astype(F32)
+        wide[i, :, H:] = grads[1, i].astype(F32)
         copies.append(pltpu.make_async_copy(wide.at[i], matrices_out.at[i // 6, i % 6], sems.at[i]))
         copies[-1].start()
     for layer in range(3):
@@ -520,19 +559,21 @@
         copy.wait()
 
 
-def group_scratch(count, shared):
-    whole = 64 if shared else B
-    spare = 16 if shared else B
+def group_scratch(kind, count):
+    whole = 64 if kind == "same" else B
+    spare = 16 if kind == "same" else B
+    small = 64 if kind == "quick" else 16
+    slots = 4 if kind == "quick" else 3
     return [
         pltpu.VMEM((2, count, B, H), BF16),
         pltpu.VMEM((count, whole, H), BF16),
         pltpu.VMEM((count, spare, H), BF16),
         pltpu.VMEM((3, count, spare // 4, H), BF16),
         pltpu.VMEM((count, 64, H), BF16),
-        pltpu.VMEM((3, count, 16, H), BF16),
-        pltpu.VMEM((count, 16, H), BF16),
-        pltpu.VMEM((4, count, 16, H), BF16),
-        pltpu.VMEM((count, 16, H), BF16),
+        pltpu.VMEM((slots, count, small, H), BF16),
+        pltpu.VMEM((count, small, H), BF16),
+        pltpu.VMEM((4, count, small, H), BF16),
+        pltpu.VMEM((count, small, H), BF16),
     ]
 
 
@@ -567,6 +608,7 @@
         pltpu.VMEM((16, H), jnp.int32),
         pltpu.VMEM((16, B), jnp.int32),
         pltpu.SemaphoreType.DMA((12,)),
+        pltpu.VMEM((2, H, B), BF16),
         pltpu.VMEM((B, B), BF16),
         pltpu.VMEM((B, B), BF16),
         pltpu.VMEM((B, B), BF16),
@@ -577,8 +619,8 @@
         pltpu.VMEM((3, 6, B, B), BF16),
         pltpu.VMEM((3, 4, B), F32),
     ]
-    for _, first, end, shared in GROUPS:
-        scratch += group_scratch(end - first, shared)
+    for kind, _, first, end in GROUPS:
+        scratch += group_scratch(kind, end - first)
     vmem = pl.BlockSpec(memory_space=pltpu.VMEM)
 
     def body(*refs):
@@ -589,7 +631,7 @@
         out_shape=(
             jax.ShapeDtypeStruct((B, B), BF16),
             jax.ShapeDtypeStruct((B, B), F32),
-            jax.ShapeDtypeStruct((18, B, B), BF16),
+            jax.ShapeDtypeStruct((2, 18, B, H), BF16),
             jax.ShapeDtypeStruct((16, B), F32),
         ),
         in_specs=[pl.BlockSpec(memory_space=pltpu.HBM)] * 9,

time: 75.8 us -> 69.4 us (0.916)
  Pallas kernels: 75 us -> 68.6 us
    pallas_call x1, Pallas kernels: 71.9 us -> 65.6 us  [local(): pl.pallas_call(body, out_shape=(jax.ShapeDtypeStruct((B, B), BF16), jax.S...]
where the time goes in v4:
time: 69.4 us; the launch traced here: 69.3 us
  Pallas kernels  68.6 us (99%)
    pallas_call x1, Pallas kernels, local(): pl.pallas_call(body, out_shape=(jax.ShapeDtypeStruct((B, B), BF16), jax.S...  65.6 us
    pallas_call x1, Pallas kernels, local(): pl.pallas_call(finish, out_shape=(jax.ShapeDtypeStruct((B, B), BF16), jax...  3.05 us

profile of v4, /device:TPU:1, one launch (start us, length us, event | category | flops | bytes accessed | tf_op | source)
XLA Modules:
  0.0 69.3 jit_solution(8402114765009434398)
XLA Ops:
  0.6 65.6 %sweep.1 = (bf16[256,256]{1,0:T(8,128)(2,1)S(1)}, f32[256,256]{1,0:T(8,128)S(1)}, bf16[2,18,256,128]{3,2,1,0:T(8,128)(2,1)S(1)}, f32[16,256]{1,0:T(8,128)S(1)}) custom-call(bf16[256,256]{1,0:T(8,128)(2,1)} %refs_0_.1, bf16[256,256]{1,0:T(8,128)(2,1)} %refs_1_.1, bf16[256,256]{1,0:T(8,128)(2,1)} %refs_2_.1, s32[4,128]{1,0:T(4,128)} %bitcast.5, ...), custom_call_target="tpu_custom_call" | custom-call | tf_op jit(solution)/shard_map/sweep/pallas_call | solution.py:629
  66.2 3.1 %finish.1 = (bf16[256,256]{1,0:T(8,128)(2,1)}, f32[256,256]{1,0:T(8,128)}, f32[3,6,256,256]{3,2,1,0:T(8,128)}, f32[3,4,256]{2,1,0:T(4,128)}) custom-call(bf16[256,256]{1,0:T(8,128)(2,1)S(1)} %get-tuple-element.8.fine_in, f32[256,256]{1,0:T(8,128)S(1)} %get-tuple-element.9.lifted_in, bf16[2,18,256,128]{3,2,1,0:T(8,128)(2,1)S(1)} %get-tuple-element.10.grads, ...), custom_call_target="tpu_custom_call" | custom-call | tf_op jit(solution)/shard_map/finish/pallas_call | solution.py:652

commit v5 on v4

--- a/solution.py
+++ b/solution.py
@@ -238,9 +238,9 @@
 def kernel(total_fine, *refs):
     inputs, (fine_out, lifted_cot, grads, gbias) = refs[:9], refs[9:13]
     (send_sems, recv_sems, onehot, samehot, act, slope, unit, scale, dys, nact, nslope, nunit, nscale,
-     table, ext, gtab, pres, csend, crecv, hsend, hback, node_in, bias_acc, bias_core, bias_slots, raw, index, load_sems, summed,
-     fine, coarse, cot, up_raw, down_raw, halo_raw, same_raw, mats, bias) = refs[13:51]
-    group_refs = refs[51:]
+     table, ext, gtab, pres, csend, crecv, hsend, hback, node_in, bias_acc, bias_core, bias_slots, raw, index, load_sems, summed, own_part,
+     fine, coarse, cot, up_raw, down_raw, halo_raw, same_raw, mats, bias) = refs[13:52]
+    group_refs = refs[52:]
     place = Place()
     posted = []
 
@@ -254,12 +254,6 @@
         posted.append(copy)
         return copy
 
-    barrier = pltpu.get_barrier_semaphore()
-    near = [place.peer(a, d) for a in ("x", "y", "z") for d in (1, 2, 3)]
-    near += [place.partner(), place.beside(1), place.beside(-1)]
-    for device in near:
-        pl.semaphore_signal(barrier, inc=1, device_id=device, device_id_type=MESH)
-
     loads = []
     for i, (src, dst) in enumerate([
         (inputs[3], up_raw), (inputs[0], fine), (inputs[1], coarse), (inputs[8], bias),
@@ -268,7 +262,16 @@
         (inputs[2], cot),
     ]):
         loads.append(pltpu.make_async_copy(src, dst, load_sems.at[i]))
-        loads[-1].start()
+    for load in loads[:5]:
+        load.start()
+
+    barrier = pltpu.get_barrier_semaphore()
+    near = [place.peer(a, d) for a in ("x", "y", "z") for d in (1, 2, 3)]
+    near += [place.partner(), place.beside(1), place.beside(-1)]
+    for device in near:
+        pl.semaphore_signal(barrier, inc=1, device_id=device, device_id_type=MESH)
+    for load in loads[5:]:
+        load.start()
 
     groups = [
         (Quick if kind == "quick" else Group)(
@@ -279,8 +282,7 @@
     edge0, (node0, layer1, layer2a, layer2b) = groups[:3], groups[3:]
 
     bias_acc[...] = jnp.zeros_like(bias_acc)
-    for load in loads[:5]:
-        load.wait()
+    loads[0].wait()
     deal(up_raw, raw, index, *UP)
 
     def step_on(*groups):
@@ -379,6 +381,8 @@
 
     for block in range(*UP):
         onehot[block] = hot_rows(block, B)
+    for load in loads[1:5]:
+        load.wait()
     sent = dot_plain(fine[...], w(0, 0)) + b(0, 0)
     table[...] = dot_plain(coarse[...], w(0, 1)).astype(BF16)
     up_sum = None
@@ -394,6 +398,9 @@
     pres[0] = dot_plain(coarse[...], w(0, 3)) + b(0, 2)
     deal(down_raw, raw, index, *DOWN)
     deal(same_raw, raw, index, *SAME)
+    place_in = index[SAME[0]:SAME[1], :]
+    moved = jnp.where(place_in < H, place_in + B, place_in - H)
+    index[SAME[0]:SAME[1], :] = jnp.where(place_in < H + B, moved, place_in)
     index[11:12, :H] = halo_raw[0:1, :]
     index[11:12, H:] = halo_raw[1:2, :]
     for block in range(*DOWN):
@@ -406,25 +413,30 @@
     pres[2] = dot_plain(fine[...], w(2, 1)) + b(2, 0)
     agg = sum_end(0, state)
     lifted = node_forward(0, coarse[...], agg, pres[0])
-    ext[H:H + B] = lifted
+    ext[:B] = lifted
     payload = dot_rows(onehot[5], lifted).astype(BF16)
     hsend[0] = payload[:H]
     hsend[1] = payload[H:]
     halo = [
-        post(hsend.at[0], ext.at[H + B:], place.beside(-1)),
-        post(hsend.at[1], ext.at[:H], place.beside(1)),
+        post(hsend.at[0], ext.at[B + H:], place.beside(-1)),
+        post(hsend.at[1], ext.at[B:B + H], place.beside(1)),
     ]
 
     pres[3] = dot_plain(lifted, w(1, 1)) + b(1, 0)
+    gtab[:B] = dot_plain(lifted, w(1, 0)).astype(BF16)
+    for block in range(*SAME):
+        own_part[block - 5] = pres[3] + dot_rows(samehot[block - 5, :B], gtab[:B])
     pres[4] = dot_plain(lifted, w(1, 3)) + b(1, 2)
     for copy in halo:
         copy.wait_recv()
-    gtab[...] = dot_plain(ext[...], w(1, 0)).astype(BF16)
+    gtab[B:] = dot_plain(ext[B:], w(1, 0)).astype(BF16)
     same_sum = None
     for block in range(*SAME):
-        message = edge_forward(block, pres[3] + dot_rows(samehot[block - 5], gtab[...]), 1)
+        message = edge_forward(
+            block, own_part[block - 5] + dot_rows(samehot[block - 5, B:], gtab[B:]), 1
+        )
         same_sum = message if same_sum is None else same_sum + message
-    mixed = node_forward(1, ext[H:H + B], same_sum.astype(BF16), pres[4])
+    mixed = node_forward(1, ext[:B], same_sum.astype(BF16), pres[4])
     nact[3] = mixed
 
     table[...] = dot_plain(mixed, w(2, 0)).astype(BF16)
@@ -466,15 +478,15 @@
         part = dot_plain(samehot[block - 5], dp.astype(BF16))
         taken = dp if taken is None else taken + dp
         back = part if back is None else back + part
-    hsend[2] = back[:H].astype(BF16)
-    hsend[3] = back[H + B:].astype(BF16)
+    hsend[2] = back[B:B + H].astype(BF16)
+    hsend[3] = back[B + H:].astype(BF16)
     returns = [
         post(hsend.at[2], hback.at[1], place.beside(-1)),
         post(hsend.at[3], hback.at[0], place.beside(1)),
     ]
-    own = back[H:H + B]
+    own = back[:B]
     step_on(layer2a, layer2b)
-    lifted = ext[H:H + B]
+    lifted = ext[:B]
     taken_half = taken.astype(BF16)
     layer1.put(1, 1.0 * dot_rows(lifted, taken_half))
     layer1.put(2, dot_rows(act[5:11].reshape(6 * B, B), dys[5:11].reshape(6 * B, B)))
@@ -493,9 +505,10 @@
 
     dz0, dq0 = node_backward(0, grad_lifted, 0.25)
     table[...] = dot_cols(dq0, w(0, 4)).astype(BF16)
-    step_on(layer2a, layer2b)
     taken = back = None
     for block in range(*UP):
+        if block == UP[1] - 1:
+            step_on(layer2a, layer2b, layer1)
         dp, db2, db1 = edge_backward(block, dot_rows(onehot[block], table[...]), 0)
         add_bias(0, db1)
         add_bias(1, db2)
@@ -511,6 +524,14 @@
     node0.put(1, dot_rows(node_in[0], dq0))
     node0.put(2, dot_rows(nact[0], dz0))
     step_on(node0)
+
+    retired, marks = [0], [0]
+
+    def retire():
+        for copy in posted[retired[0]:marks[-1]]:
+            copy.wait_send()
+        retired[0] = marks[-1]
+        marks.append(len(posted))
 
     def bias_step(step):
         for copy in bias_waits:
@@ -535,10 +556,12 @@
         step_on(*edge0, node0, layer1, layer2a, layer2b)
         if step < 4:
             bias_step(step)
+        retire()
     assert all(group.step == 8 for group in groups)
     assert len(posted) <= COPIES
-    for copy in posted:
-        copy.wait_send()
+    retire()
+    retire()
+    assert retired[0] == len(posted)
 
 
 def finish(fine_in, lifted_in, grads, gbias, fine_out, lifted_out, matrices_out, biases_out, wide, sems):
@@ -609,6 +632,7 @@
         pltpu.VMEM((16, B), jnp.int32),
         pltpu.SemaphoreType.DMA((12,)),
         pltpu.VMEM((2, H, B), BF16),
+        pltpu.VMEM((6, B, B), F32),
         pltpu.VMEM((B, B), BF16),
         pltpu.VMEM((B, B), BF16),
         pltpu.VMEM((B, B), BF16),

time: 69.4 us -> 67.5 us (0.973)
  Pallas kernels: 68.6 us -> 66.7 us
    pallas_call x1, Pallas kernels: 65.6 us -> 63.6 us  [local(): pl.pallas_call(body, out_shape=(jax.ShapeDtypeStruct((B, B), BF16), jax.S...]
where the time goes in v5:
time: 67.5 us; the launch traced here: 67.3 us
  Pallas kernels  66.7 us (99%)
    pallas_call x1, Pallas kernels, local(): pl.pallas_call(body, out_shape=(jax.ShapeDtypeStruct((B, B), BF16), jax.S...  63.6 us
    pallas_call x1, Pallas kernels, local(): pl.pallas_call(finish, out_shape=(jax.ShapeDtypeStruct((B, B), BF16), jax...  3.05 us

profile of v5, /device:TPU:1, one launch (start us, length us, event | category | flops | bytes accessed | tf_op | source)
XLA Modules:
  0.0 67.3 jit_solution(12639895193651450804)
XLA Ops:
  0.6 63.6 %sweep.1 = (bf16[256,256]{1,0:T(8,128)(2,1)S(1)}, f32[256,256]{1,0:T(8,128)S(1)}, bf16[2,18,256,128]{3,2,1,0:T(8,128)(2,1)S(1)}, f32[16,256]{1,0:T(8,128)S(1)}) custom-call(bf16[256,256]{1,0:T(8,128)(2,1)} %refs_0_.1, bf16[256,256]{1,0:T(8,128)(2,1)} %refs_1_.1, bf16[256,256]{1,0:T(8,128)(2,1)} %refs_2_.1, s32[4,128]{1,0:T(4,128)} %bitcast.5, ...), custom_call_target="tpu_custom_call" | custom-call | tf_op jit(solution)/shard_map/sweep/pallas_call | solution.py:653
  64.3 3.1 %finish.1 = (bf16[256,256]{1,0:T(8,128)(2,1)}, f32[256,256]{1,0:T(8,128)}, f32[3,6,256,256]{3,2,1,0:T(8,128)}, f32[3,4,256]{2,1,0:T(4,128)}) custom-call(bf16[256,256]{1,0:T(8,128)(2,1)S(1)} %get-tuple-element.8.fine_in, f32[256,256]{1,0:T(8,128)S(1)} %get-tuple-element.9.lifted_in, bf16[2,18,256,128]{3,2,1,0:T(8,128)(2,1)S(1)} %get-tuple-element.10.grads, ...), custom_call_target="tpu_custom_call" | custom-call | tf_op jit(solution)/shard_map/finish/pallas_call | solution.py:676

commit v6 on v5

--- a/solution.py
+++ b/solution.py
@@ -13,8 +13,11 @@
 B = 256
 H = 128
 UP, DOWN, SAME = (0, 2), (2, 5), (5, 11)
-COPIES = 160
-PIECES = 4
+BATCHES = 58
+SENDS = 3
+UNIT = 4096
+RULER = 512
+PIECES = 2
 GROUPS = (
     ("quick", ("x", "y", "z"), 0, 1),
     ("quick", ("z", "x", "y"), 1, 2),
@@ -62,6 +65,15 @@
     return jnp.sum(x, axis=0, keepdims=True)
 
 
+class Batch:
+    def __init__(self, sem, ruler):
+        self.sem, self.ruler, self.size = sem, ruler, 0
+
+    def wait(self):
+        span = self.ruler.at[:self.size // UNIT]
+        pltpu.make_async_copy(span, span, self.sem).wait()
+
+
 class Group:
     def __init__(self, post, place, axes, rows, shared, refs, out):
         self.shared = shared
@@ -69,17 +81,19 @@
         self.g, self.rc, self.s1, self.r1, self.s2, self.r2, self.s3, self.r3, self.s4 = refs
         self.count = rows.stop - rows.start
         self.step = 0
-        self.copies = []
+        self.batch = None
 
     def put(self, i, value):
         half = value.astype(BF16)
         self.g[0, i] = half[:, :H]
         self.g[1, i] = half[:, H:]
 
+    def send(self, src, dst, device):
+        self.batch = self.post(src, dst, device, self.batch)
+
     def landed(self):
-        for copy in self.copies:
-            copy.wait_recv()
-        self.copies = []
+        self.batch.wait()
+        self.batch = None
 
     def advance(self):
         getattr(self, "step%d" % self.step)()
@@ -91,7 +105,7 @@
     def step0(self):
         other = 1 - self.place.core
         src = self.g.at[other, :, self.quarter(), :] if self.shared else self.g.at[other]
-        self.copies = [self.post(src, self.rc, self.place.partner())]
+        self.send(src, self.rc, self.place.partner())
 
     def step1(self):
         self.landed()
@@ -112,7 +126,7 @@
         for d in (1, 2, 3):
             to = lax.rem(at + d, 4)
             rows = pl.ds(pl.multiple_of(to * size, size), size)
-            self.copies.append(self.post(src.at[:, rows, :], landing.at[d - 1], self.place.peer(axis, d)))
+            self.send(src.at[:, rows, :], landing.at[d - 1], self.place.peer(axis, d))
 
     def gather_sum(self, axis, size, src, landing, out):
         at = self.place.at(axis)
@@ -136,7 +150,7 @@
     def share(self, axis, src, slots):
         at = self.place.at(axis)
         for d in (1, 2, 3):
-            self.copies.append(self.post(src, slots.at[at], self.place.peer(axis, d)))
+            self.send(src, slots.at[at], self.place.peer(axis, d))
         slots[at] = src[...]
 
     def slot_sum(self, slots, out):
@@ -153,7 +167,7 @@
         rows = pl.ds(pl.multiple_of(start, 16), 16)
         spot = self.out.at[self.place.core, self.rows, rows, :]
         for d in (1, 2, 3):
-            self.copies.append(self.post(self.s4, spot, self.place.peer(self.axes[1], d)))
+            self.send(self.s4, spot, self.place.peer(self.axes[1], d))
         for i in range(self.count):
             self.out[self.place.core, self.rows.start + i, rows, :] = self.s4[i]
 
@@ -161,12 +175,12 @@
         self.landed()
         spot = self.out.at[self.place.core, self.rows, self.quarter(), :]
         for d in (1, 2, 3):
-            self.copies.append(self.post(spot, spot, self.place.peer(self.axes[0], d)))
+            self.send(spot, spot, self.place.peer(self.axes[0], d))
 
     def step6(self):
         self.landed()
         spot = self.out.at[self.place.core, self.rows, :, :]
-        self.copies = [self.post(spot, spot, self.place.partner())]
+        self.send(spot, spot, self.place.partner())
 
     def step7(self):
         self.landed()
@@ -188,7 +202,7 @@
         self.slot_sum(self.r3, self.s4)
         spot = self.out.at[self.place.core, self.rows, self.quarter(), :]
         for d in (1, 2, 3):
-            self.copies.append(self.post(self.s4, spot, self.place.peer(self.axes[0], d)))
+            self.send(self.s4, spot, self.place.peer(self.axes[0], d))
         for i in range(self.count):
             self.out[self.place.core, self.rows.start + i, self.quarter(), :] = self.s4[i]
         self.step = 5
@@ -238,22 +252,31 @@
 def kernel(total_fine, *refs):
     inputs, (fine_out, lifted_cot, grads, gbias) = refs[:9], refs[9:13]
     (send_sems, recv_sems, onehot, samehot, act, slope, unit, scale, dys, nact, nslope, nunit, nscale,
-     table, ext, gtab, pres, csend, crecv, hsend, hback, node_in, bias_acc, bias_core, bias_slots, raw, index, load_sems, summed, own_part,
-     fine, coarse, cot, up_raw, down_raw, halo_raw, same_raw, mats, bias) = refs[13:52]
-    group_refs = refs[52:]
+     table, ext, gtab, pres, csend, crecv, hsend, hback, node_in, bias_acc, bias_core, bias_slots, raw, index, load_sems, summed, own_part, ruler,
+     fine, coarse, cot, up_raw, down_raw, halo_raw, same_raw, mats, bias) = refs[13:53]
+    group_refs = refs[53:]
     place = Place()
-    posted = []
-
-    def post(src, dst, device):
-        i = len(posted)
-        copy = pltpu.make_async_remote_copy(
-            src_ref=src, dst_ref=dst, send_sem=send_sems.at[i], recv_sem=recv_sems.at[i],
+    batches = []
+    leaving = []
+
+    def next_sends():
+        leaving.append(Batch(send_sems.at[len(leaving)], ruler))
+
+    def post(src, dst, device, batch=None):
+        if batch is None:
+            batch = Batch(recv_sems.at[len(batches)], ruler)
+            batches.append(batch)
+        pltpu.make_async_remote_copy(
+            src_ref=src, dst_ref=dst, send_sem=leaving[-1].sem, recv_sem=batch.sem,
             device_id=device, device_id_type=MESH,
-        )
-        copy.start()
-        posted.append(copy)
-        return copy
-
+        ).start()
+        size = math.prod(dst.shape) * dst.dtype.itemsize
+        assert size % UNIT == 0
+        batch.size += size
+        leaving[-1].size += size
+        return batch
+
+    next_sends()
     loads = []
     for i, (src, dst) in enumerate([
         (inputs[3], up_raw), (inputs[0], fine), (inputs[1], coarse), (inputs[8], bias),
@@ -352,31 +375,33 @@
         two = (lax.rem(place.gx + 2 * odd + 3, 4), place.gy)
         waits = []
         for i in range(PIECES):
+            batch = None
             for side, device in ((0, one), (1, two)):
-                waits.append(post(csend.at[first, side, piece(i)], crecv.at[first, side, piece(i)], device))
+                batch = post(csend.at[first, side, piece(i)], crecv.at[first, side, piece(i)], device, batch)
+            waits.append(batch)
         return waits, one, two
 
-    def sum_pieces(at, waits, out, then):
-        for i in range(PIECES):
-            for side in (0, 1):
-                waits[2 * i + side].wait_recv()
-                both = csend[at, side, piece(i)].astype(F32) + crecv[at, side, piece(i)].astype(F32)
-                out[side, piece(i)] = both.astype(BF16)
-                then(i, side)
+    def add_piece(at, i, side):
+        both = csend[at, side, piece(i)].astype(F32) + crecv[at, side, piece(i)].astype(F32)
+        return both.astype(BF16)
 
     def sum_middle(first, state):
         waits, one, two = state
         later = []
-
-        def send_on(i, side):
-            device = (two, one)[side]
-            later.append(post(csend.at[first + 1, side, piece(i)], crecv.at[first + 1, side, piece(i)], device))
-
-        sum_pieces(first, waits, csend.at[first + 1], send_on)
+        for i in range(PIECES):
+            waits[i].wait()
+            batch = None
+            for side, device in ((0, two), (1, one)):
+                csend[first + 1, side, piece(i)] = add_piece(first, i, side)
+                batch = post(csend.at[first + 1, side, piece(i)], crecv.at[first + 1, side, piece(i)], device, batch)
+            later.append(batch)
         return later
 
     def sum_end(first, waits):
-        sum_pieces(first + 1, waits, summed, lambda i, side: None)
+        for i in range(PIECES):
+            waits[i].wait()
+            for side in (0, 1):
+                summed[side, piece(i)] = add_piece(first + 1, i, side)
         return summed[...].reshape(B, B)
 
     for block in range(*UP):
@@ -417,18 +442,15 @@
     payload = dot_rows(onehot[5], lifted).astype(BF16)
     hsend[0] = payload[:H]
     hsend[1] = payload[H:]
-    halo = [
-        post(hsend.at[0], ext.at[B + H:], place.beside(-1)),
-        post(hsend.at[1], ext.at[B:B + H], place.beside(1)),
-    ]
+    halo = post(hsend.at[0], ext.at[B + H:], place.beside(-1))
+    post(hsend.at[1], ext.at[B:B + H], place.beside(1), halo)
 
     pres[3] = dot_plain(lifted, w(1, 1)) + b(1, 0)
     gtab[:B] = dot_plain(lifted, w(1, 0)).astype(BF16)
     for block in range(*SAME):
         own_part[block - 5] = pres[3] + dot_rows(samehot[block - 5, :B], gtab[:B])
     pres[4] = dot_plain(lifted, w(1, 3)) + b(1, 2)
-    for copy in halo:
-        copy.wait_recv()
+    halo.wait()
     gtab[B:] = dot_plain(ext[B:], w(1, 0)).astype(BF16)
     same_sum = None
     for block in range(*SAME):
@@ -480,10 +502,8 @@
         back = part if back is None else back + part
     hsend[2] = back[B:B + H].astype(BF16)
     hsend[3] = back[B + H:].astype(BF16)
-    returns = [
-        post(hsend.at[2], hback.at[1], place.beside(-1)),
-        post(hsend.at[3], hback.at[0], place.beside(1)),
-    ]
+    returns = post(hsend.at[2], hback.at[1], place.beside(-1))
+    post(hsend.at[3], hback.at[0], place.beside(1), returns)
     own = back[:B]
     step_on(layer2a, layer2b)
     lifted = ext[:B]
@@ -494,8 +514,8 @@
     layer1.put(4, dot_rows(node_in[1], dq1))
     layer1.put(5, dot_rows(nact[1], dz1))
     grad_lifted = pres[0] + dot_cols(taken_half, w(1, 1))
-    for copy in returns:
-        copy.wait_recv()
+    returns.wait()
+    next_sends()
     own += dot_plain(onehot[5], hback[...].reshape(B, B))
     own_half = own.astype(BF16)
     grad_lifted += dot_cols(own_half, w(1, 0))
@@ -519,24 +539,15 @@
     edge0[1].put(0, dot_rows(coarse[...], back.astype(BF16)))
     edge0[2].put(0, dot_rows(act[0:2].reshape(2 * B, B), dys[0:2].reshape(2 * B, B)))
     step_on(*edge0)
-    bias_waits = [post(bias_acc, bias_core, place.partner())]
+    bias_batch = [post(bias_acc, bias_core, place.partner())]
     node0.put(0, dot_rows(coarse[...], dq0))
     node0.put(1, dot_rows(node_in[0], dq0))
     node0.put(2, dot_rows(nact[0], dz0))
     step_on(node0)
 
-    retired, marks = [0], [0]
-
-    def retire():
-        for copy in posted[retired[0]:marks[-1]]:
-            copy.wait_send()
-        retired[0] = marks[-1]
-        marks.append(len(posted))
-
     def bias_step(step):
-        for copy in bias_waits:
-            copy.wait_recv()
-        bias_waits.clear()
+        bias_batch.pop().wait()
+        batch = None
         if step == 0:
             total = bias_acc[...] + bias_core[...]
         else:
@@ -550,34 +561,39 @@
         bias_slots[step, at] = total
         for d in (1, 2, 3):
             spot = bias_slots.at[step, at]
-            bias_waits.append(post(spot, spot, place.peer(axis, d)))
+            batch = post(spot, spot, place.peer(axis, d), batch)
+        bias_batch.append(batch)
 
     for step in range(6):
         step_on(*edge0, node0, layer1, layer2a, layer2b)
         if step < 4:
             bias_step(step)
-        retire()
+        if step == 2:
+            leaving[0].wait()
+            next_sends()
+        if step == 3:
+            leaving[1].wait()
     assert all(group.step == 8 for group in groups)
-    assert len(posted) <= COPIES
-    retire()
-    retire()
-    assert retired[0] == len(posted)
+    leaving[2].wait()
+    assert len(batches) == BATCHES and len(leaving) == SENDS
+    assert max(batch.size for batch in batches + leaving) <= RULER * UNIT
 
 
 def finish(fine_in, lifted_in, grads, gbias, fine_out, lifted_out, matrices_out, biases_out, wide, sems):
     copies = [
-        pltpu.make_async_copy(fine_in, fine_out, sems.at[18]),
-        pltpu.make_async_copy(lifted_in, lifted_out, sems.at[19]),
+        pltpu.make_async_copy(fine_in, fine_out, sems.at[3]),
+        pltpu.make_async_copy(lifted_in, lifted_out, sems.at[4]),
     ]
     for copy in copies:
         copy.start()
     for i in range(18):
+        layer = i // 6
         wide[i, :, :H] = grads[0, i].astype(F32)
         wide[i, :, H:] = grads[1, i].astype(F32)
-        copies.append(pltpu.make_async_copy(wide.at[i], matrices_out.at[i // 6, i % 6], sems.at[i]))
-        copies[-1].start()
+        pltpu.make_async_copy(wide.at[i], matrices_out.at[layer, i % 6], sems.at[layer]).start()
     for layer in range(3):
         biases_out[layer] = gbias[4 * layer:4 * layer + 4, :]
+        copies.append(pltpu.make_async_copy(wide.at[6 * layer:6 * layer + 6], matrices_out.at[layer], sems.at[layer]))
     for copy in copies:
         copy.wait()
 
@@ -603,8 +619,8 @@
 def local(fine_state, coarse_state, up_target, down_source, halo_lists, same_source, matrices, biases, fine_cotangent):
     total_fine = fine_state.shape[0] * lax.axis_size("gx") * lax.axis_size("gy")
     scratch = [
-        pltpu.SemaphoreType.DMA((COPIES,)),
-        pltpu.SemaphoreType.DMA((COPIES,)),
+        pltpu.SemaphoreType.DMA((SENDS,)),
+        pltpu.SemaphoreType.DMA((BATCHES,)),
         pltpu.VMEM((6, B, B), BF16),
         pltpu.VMEM((6, 2 * B, B), BF16),
         pltpu.VMEM((11, B, B), BF16),
@@ -633,6 +649,7 @@
         pltpu.SemaphoreType.DMA((12,)),
         pltpu.VMEM((2, H, B), BF16),
         pltpu.VMEM((6, B, B), F32),
+        pltpu.VMEM((RULER, 16, H), BF16),
         pltpu.VMEM((B, B), BF16),
         pltpu.VMEM((B, B), BF16),
         pltpu.VMEM((B, B), BF16),
@@ -683,7 +700,7 @@
         ),
         in_specs=[vmem] * 4,
         out_specs=(hbm, hbm, hbm, vmem),
-        scratch_shapes=[pltpu.VMEM((18, B, B), F32), pltpu.SemaphoreType.DMA((20,))],
+        scratch_shapes=[pltpu.VMEM((18, B, B), F32), pltpu.SemaphoreType.DMA((5,))],
         compiler_params=pltpu.CompilerParams(vmem_limit_bytes=16 << 20),
         name="finish",
     )(fine_out, lifted, grads, gbias)

time: 67.5 us -> 65.6 us (0.972)
  Pallas kernels: 66.7 us -> 64.8 us
    pallas_call x1, Pallas kernels: 63.6 us -> 61.9 us  [local(): pl.pallas_call(body, out_shape=(jax.ShapeDtypeStruct((B, B), BF16), jax.S...]
where the time goes in v6:
time: 65.6 us; the launch traced here: 65.4 us
  Pallas kernels  64.8 us (99%)
    pallas_call x1, Pallas kernels, local(): pl.pallas_call(body, out_shape=(jax.ShapeDtypeStruct((B, B), BF16), jax.S...  61.9 us
    pallas_call x1, Pallas kernels, local(): pl.pallas_call(finish, out_shape=(jax.ShapeDtypeStruct((B, B), BF16), jax...  2.92 us

profile of v6, /device:TPU:1, one launch (start us, length us, event | category | flops | bytes accessed | tf_op | source)
XLA Modules:
  0.0 65.4 jit_solution(7954694013204043145)
XLA Ops:
  0.6 61.9 %sweep.1 = (bf16[256,256]{1,0:T(8,128)(2,1)S(1)}, f32[256,256]{1,0:T(8,128)S(1)}, bf16[2,18,256,128]{3,2,1,0:T(8,128)(2,1)S(1)}, f32[16,256]{1,0:T(8,128)S(1)}) custom-call(bf16[256,256]{1,0:T(8,128)(2,1)} %refs_0_.1, bf16[256,256]{1,0:T(8,128)(2,1)} %refs_1_.1, bf16[256,256]{1,0:T(8,128)(2,1)} %refs_2_.1, s32[4,128]{1,0:T(4,128)} %bitcast.5, ...), custom_call_target="tpu_custom_call" | custom-call | tf_op jit(solution)/shard_map/sweep/pallas_call | solution.py:670
  62.5 2.9 %finish.1 = (bf16[256,256]{1,0:T(8,128)(2,1)}, f32[256,256]{1,0:T(8,128)}, f32[3,6,256,256]{3,2,1,0:T(8,128)}, f32[3,4,256]{2,1,0:T(4,128)}) custom-call(bf16[256,256]{1,0:T(8,128)(2,1)S(1)} %get-tuple-element.8.fine_in, f32[256,256]{1,0:T(8,128)S(1)} %get-tuple-element.9.lifted_in, bf16[2,18,256,128]{3,2,1,0:T(8,128)(2,1)S(1)} %get-tuple-element.10.grads, ...), custom_call_target="tpu_custom_call" | custom-call | tf_op jit(solution)/shard_map/finish/pallas_call | solution.py:693

commit v7 on v6

--- a/solution.py
+++ b/solution.py
@@ -13,15 +13,15 @@
 B = 256
 H = 128
 UP, DOWN, SAME = (0, 2), (2, 5), (5, 11)
-BATCHES = 58
+BATCHES = 66
 SENDS = 3
 UNIT = 4096
 RULER = 512
-PIECES = 2
+PIECES = 4
 GROUPS = (
     ("quick", ("x", "y", "z"), 0, 1),
     ("quick", ("z", "x", "y"), 1, 2),
-    ("quick", ("y", "z", "x"), 2, 3),
+    ("quick", ("x", "z", "y"), 2, 3),
     ("same", ("y", "x", "z"), 3, 6),
     ("same", ("y", "z", "x"), 6, 12),
     ("fine", ("x", "z", "y"), 12, 15),
@@ -41,10 +41,10 @@
     return lax.dot_general(a, b, (((1,), (1,)), ((), ())), preferred_element_type=F32)
 
 
-def silu_parts(x):
-    gate = 0.5 * jnp.tanh(0.5 * x) + 0.5
-    active = x * gate
-    return active, gate + active * (1.0 - gate)
+def silu_parts(u):
+    twice = 1.0 + jnp.tanh(u)
+    active = u * twice
+    return active, 0.5 * (twice + active * (2.0 - twice))
 
 
 def row_mean(x):
@@ -345,7 +345,7 @@
 
     def node_forward(layer, state, agg, pre):
         node_in[layer] = agg
-        active, slope_now = silu_parts(pre + dot_plain(agg, w(layer, 4)))
+        active, slope_now = silu_parts(0.5 * (pre + dot_plain(agg, w(layer, 4))))
         half = active.astype(BF16)
         nact[layer] = half
         nslope[layer] = slope_now.astype(BF16)
@@ -408,8 +408,8 @@
         onehot[block] = hot_rows(block, B)
     for load in loads[1:5]:
         load.wait()
-    sent = dot_plain(fine[...], w(0, 0)) + b(0, 0)
-    table[...] = dot_plain(coarse[...], w(0, 1)).astype(BF16)
+    sent = 0.5 * (dot_plain(fine[...], w(0, 0)) + b(0, 0))
+    table[...] = (0.5 * dot_plain(coarse[...], w(0, 1))).astype(BF16)
     up_sum = None
     for block in range(*UP):
         message = edge_forward(block, sent + dot_rows(onehot[block], table[...]), 0)
@@ -435,7 +435,7 @@
     for block in range(*SAME):
         samehot[block - 5] = hot_rows(block, 2 * B)
     pres[1] = dot_plain(fine[...], w(2, 3)) + b(2, 2)
-    pres[2] = dot_plain(fine[...], w(2, 1)) + b(2, 0)
+    pres[2] = 0.5 * (dot_plain(fine[...], w(2, 1)) + b(2, 0))
     agg = sum_end(0, state)
     lifted = node_forward(0, coarse[...], agg, pres[0])
     ext[:B] = lifted
@@ -445,13 +445,13 @@
     halo = post(hsend.at[0], ext.at[B + H:], place.beside(-1))
     post(hsend.at[1], ext.at[B:B + H], place.beside(1), halo)
 
-    pres[3] = dot_plain(lifted, w(1, 1)) + b(1, 0)
-    gtab[:B] = dot_plain(lifted, w(1, 0)).astype(BF16)
+    pres[3] = 0.5 * (dot_plain(lifted, w(1, 1)) + b(1, 0))
+    gtab[:B] = (0.5 * dot_plain(lifted, w(1, 0))).astype(BF16)
     for block in range(*SAME):
         own_part[block - 5] = pres[3] + dot_rows(samehot[block - 5, :B], gtab[:B])
     pres[4] = dot_plain(lifted, w(1, 3)) + b(1, 2)
     halo.wait()
-    gtab[B:] = dot_plain(ext[B:], w(1, 0)).astype(BF16)
+    gtab[B:] = (0.5 * dot_plain(ext[B:], w(1, 0))).astype(BF16)
     same_sum = None
     for block in range(*SAME):
         message = edge_forward(
@@ -461,7 +461,7 @@
     mixed = node_forward(1, ext[:B], same_sum.astype(BF16), pres[4])
     nact[3] = mixed
 
-    table[...] = dot_plain(mixed, w(2, 0)).astype(BF16)
+    table[...] = (0.5 * dot_plain(mixed, w(2, 0))).astype(BF16)
     down_sum = None
     for block in range(*DOWN):
         message = edge_forward(block, pres[2] + dot_rows(onehot[block], table[...]), 2)

time: 65.6 us -> 65 us (level)
  no operation moved by 1% of the time
where the time goes in v7:
time: 65 us; the launch traced here: 64.8 us
  Pallas kernels  64.2 us (99%)
    pallas_call x1, Pallas kernels, local(): pl.pallas_call(body, out_shape=(jax.ShapeDtypeStruct((B, B), BF16), jax.S...  61.3 us
    pallas_call x1, Pallas kernels, local(): pl.pallas_call(finish, out_shape=(jax.ShapeDtypeStruct((B, B), BF16), jax...  2.92 us

profile of v7, /device:TPU:1, one launch (start us, length us, event | category | flops | bytes accessed | tf_op | source)
XLA Modules:
  0.0 64.8 jit_solution(14709521968428375405)
XLA Ops:
  0.6 61.3 %sweep.1 = (bf16[256,256]{1,0:T(8,128)(2,1)S(1)}, f32[256,256]{1,0:T(8,128)S(1)}, bf16[2,18,256,128]{3,2,1,0:T(8,128)(2,1)S(1)}, f32[16,256]{1,0:T(8,128)S(1)}) custom-call(bf16[256,256]{1,0:T(8,128)(2,1)} %refs_0_.1, bf16[256,256]{1,0:T(8,128)(2,1)} %refs_1_.1, bf16[256,256]{1,0:T(8,128)(2,1)} %refs_2_.1, s32[4,128]{1,0:T(4,128)} %bitcast.5, ...), custom_call_target="tpu_custom_call" | custom-call | tf_op jit(solution)/shard_map/sweep/pallas_call | solution.py:670
  61.9 2.9 %finish.1 = (bf16[256,256]{1,0:T(8,128)(2,1)}, f32[256,256]{1,0:T(8,128)}, f32[3,6,256,256]{3,2,1,0:T(8,128)}, f32[3,4,256]{2,1,0:T(4,128)}) custom-call(bf16[256,256]{1,0:T(8,128)(2,1)S(1)} %get-tuple-element.8.fine_in, f32[256,256]{1,0:T(8,128)S(1)} %get-tuple-element.9.lifted_in, bf16[2,18,256,128]{3,2,1,0:T(8,128)(2,1)S(1)} %get-tuple-element.10.grads, ...), custom_call_target="tpu_custom_call" | custom-call | tf_op jit(solution)/shard_map/finish/pallas_call | solution.py:693

commit v8 on v7

--- a/solution.py
+++ b/solution.py
@@ -13,11 +13,11 @@
 B = 256
 H = 128
 UP, DOWN, SAME = (0, 2), (2, 5), (5, 11)
-BATCHES = 66
+BATCHES = 82
 SENDS = 3
 UNIT = 4096
 RULER = 512
-PIECES = 4
+PIECES = 8
 GROUPS = (
     ("quick", ("x", "y", "z"), 0, 1),
     ("quick", ("z", "x", "y"), 1, 2),

time: 65 us -> 64.9 us (level)
  no operation moved by 1% of the time
where the time goes in v8:
time: 64.9 us; the launch traced here: 64.8 us
  Pallas kernels  64.1 us (99%)
    pallas_call x1, Pallas kernels, local(): pl.pallas_call(body, out_shape=(jax.ShapeDtypeStruct((B, B), BF16), jax.S...  61.2 us
    pallas_call x1, Pallas kernels, local(): pl.pallas_call(finish, out_shape=(jax.ShapeDtypeStruct((B, B), BF16), jax...  2.92 us

profile of v8, /device:TPU:1, one launch (start us, length us, event | category | flops | bytes accessed | tf_op | source)
XLA Modules:
  0.0 64.8 jit_solution(17716690815856868525)
XLA Ops:
  0.6 61.2 %sweep.1 = (bf16[256,256]{1,0:T(8,128)(2,1)S(1)}, f32[256,256]{1,0:T(8,128)S(1)}, bf16[2,18,256,128]{3,2,1,0:T(8,128)(2,1)S(1)}, f32[16,256]{1,0:T(8,128)S(1)}) custom-call(bf16[256,256]{1,0:T(8,128)(2,1)} %refs_0_.1, bf16[256,256]{1,0:T(8,128)(2,1)} %refs_1_.1, bf16[256,256]{1,0:T(8,128)(2,1)} %refs_2_.1, s32[4,128]{1,0:T(4,128)} %bitcast.5, ...), custom_call_target="tpu_custom_call" | custom-call | tf_op jit(solution)/shard_map/sweep/pallas_call | solution.py:670
  61.8 2.9 %finish.1 = (bf16[256,256]{1,0:T(8,128)(2,1)}, f32[256,256]{1,0:T(8,128)}, f32[3,6,256,256]{3,2,1,0:T(8,128)}, f32[3,4,256]{2,1,0:T(4,128)}) custom-call(bf16[256,256]{1,0:T(8,128)(2,1)S(1)} %get-tuple-element.8.fine_in, f32[256,256]{1,0:T(8,128)S(1)} %get-tuple-element.9.lifted_in, bf16[2,18,256,128]{3,2,1,0:T(8,128)(2,1)S(1)} %get-tuple-element.10.grads, ...), custom_call_target="tpu_custom_call" | custom-call | tf_op jit(solution)/shard_map/finish/pallas_call | solution.py:693

commit v9 on v6

--- a/solution.py
+++ b/solution.py
@@ -13,15 +13,15 @@
 B = 256
 H = 128
 UP, DOWN, SAME = (0, 2), (2, 5), (5, 11)
-BATCHES = 58
+BATCHES = 82
 SENDS = 3
 UNIT = 4096
 RULER = 512
-PIECES = 2
+PIECES = 8
 GROUPS = (
     ("quick", ("x", "y", "z"), 0, 1),
     ("quick", ("z", "x", "y"), 1, 2),
-    ("quick", ("y", "z", "x"), 2, 3),
+    ("quick", ("x", "z", "y"), 2, 3),
     ("same", ("y", "x", "z"), 3, 6),
     ("same", ("y", "z", "x"), 6, 12),
     ("fine", ("x", "z", "y"), 12, 15),

time: 65.6 us -> 64.9 us (0.989)
  Pallas kernels: 64.8 us -> 64.1 us
    pallas_call x1, Pallas kernels: 61.9 us -> 61.2 us  [local(): pl.pallas_call(body, out_shape=(jax.ShapeDtypeStruct((B, B), BF16), jax.S...]
where the time goes in v9:
time: 64.9 us; the launch traced here: 64.8 us
  Pallas kernels  64.1 us (99%)
    pallas_call x1, Pallas kernels, local(): pl.pallas_call(body, out_shape=(jax.ShapeDtypeStruct((B, B), BF16), jax.S...  61.2 us
    pallas_call x1, Pallas kernels, local(): pl.pallas_call(finish, out_shape=(jax.ShapeDtypeStruct((B, B), BF16), jax...  2.92 us

profile of v9, /device:TPU:1, one launch (start us, length us, event | category | flops | bytes accessed | tf_op | source)
XLA Modules:
  0.0 64.8 jit_solution(2983992416278148941)
XLA Ops:
  0.6 61.2 %sweep.1 = (bf16[256,256]{1,0:T(8,128)(2,1)S(1)}, f32[256,256]{1,0:T(8,128)S(1)}, bf16[2,18,256,128]{3,2,1,0:T(8,128)(2,1)S(1)}, f32[16,256]{1,0:T(8,128)S(1)}) custom-call(bf16[256,256]{1,0:T(8,128)(2,1)} %refs_0_.1, bf16[256,256]{1,0:T(8,128)(2,1)} %refs_1_.1, bf16[256,256]{1,0:T(8,128)(2,1)} %refs_2_.1, s32[4,128]{1,0:T(4,128)} %bitcast.5, ...), custom_call_target="tpu_custom_call" | custom-call | tf_op jit(solution)/shard_map/sweep/pallas_call | solution.py:670
  61.9 2.9 %finish.1 = (bf16[256,256]{1,0:T(8,128)(2,1)}, f32[256,256]{1,0:T(8,128)}, f32[3,6,256,256]{3,2,1,0:T(8,128)}, f32[3,4,256]{2,1,0:T(4,128)}) custom-call(bf16[256,256]{1,0:T(8,128)(2,1)S(1)} %get-tuple-element.8.fine_in, f32[256,256]{1,0:T(8,128)S(1)} %get-tuple-element.9.lifted_in, bf16[2,18,256,128]{3,2,1,0:T(8,128)(2,1)S(1)} %get-tuple-element.10.grads, ...), custom_call_target="tpu_custom_call" | custom-call | tf_op jit(solution)/shard_map/finish/pallas_call | solution.py:693
